TPU v7x, 128 devices: a whole 4x4x4 slice. The times are simulated.
128 devices in a mesh: chan: 16 (over y, z), win: 8 (over x, core).
Axes of the slice: x: 4, y: 4, z: 4, core: 2. Of those that a mesh axis runs over, the one named last changes fastest.
Arguments:
- spectra: bfloat16 [768, 32, 2, 1024], P('chan', 'win'), may hold values from -120 to 120
- sources: int32 [4], replicated, may hold values from 0 to 767
- bin_rows: int32 [4, 16, 32, 3], P(None, 'chan'), may hold values from -1 to 47, as said below
Outputs:
- stacked: float32 [4, 32, 4096], P(None, 'chan', 'win')
Inputs may be any that keep to these rules, and one draw needn't show every extreme that they name: `bin_rows`: for every step and every index d of chan, the entries name each of that device's 48 local receiver rows exactly once; within a bin the used slots come first and the rest are -1. In each step one bin uses all 3 slots on every device.
All inputs are finite; a program needn't handle non-finite values.
Results may differ from a plain program's by a relative error of at most 0.0099.
Values may be sent and summed in bfloat16 or wider, within the bound.
No kernel may reach another device: no remote copies, remote signals or barrier semaphores. Data moves between devices by JAX's collectives and lax.ppermute only.
A program may use at most 768 MiB of HBM per device.

v0:
```python
import jax
import jax.numpy as jnp
from jax import lax
from jax.sharding import PartitionSpec as P

F = 1024
F0 = 32
NFFT = 8192
LMAX = 2048
HW = 32
NBINS = 32
MOST = 3
LAGS = 4096


epsilon_amp = 1e-06
phase_floor = 0.1


def broadcast(block, axis, source):
    block = jnp.where(lax.axis_index(axis) == source, block, jnp.zeros_like(block))
    return lax.psum(block, axis)


def band_matrix():
    index = jnp.arange(F, dtype=jnp.int32)
    inside = jnp.abs(index[:, None] - index[None, :]) <= HW
    return inside.astype(jnp.float32) / (2 * HW + 1)


def whiten(spectra):
    real_part = spectra[:, :, 0, :].astype(jnp.float32)
    imag_part = spectra[:, :, 1, :].astype(jnp.float32)
    amplitude = jnp.sqrt(real_part * real_part + imag_part * imag_part)
    smooth = jnp.dot(amplitude.reshape(-1, F), band_matrix(), precision=lax.Precision.HIGHEST)
    smooth = smooth.reshape(amplitude.shape) + epsilon_amp
    return jnp.stack([real_part / smooth, imag_part / smooth], axis=2).astype(jnp.bfloat16)


def cross_spectra(white, source):
    white_real = white[..., 0, :].astype(jnp.float32)
    white_imag = white[..., 1, :].astype(jnp.float32)
    source_real = source[..., 0, :].astype(jnp.float32)
    source_imag = source[..., 1, :].astype(jnp.float32)
    cross_real = white_real * source_real + white_imag * source_imag
    cross_imag = white_imag * source_real - white_real * source_imag
    return jnp.concatenate([cross_real, cross_imag], axis=-1).astype(jnp.bfloat16)


def lag_table(first_lag, lag_count):
    frequency = F0 + jnp.arange(F, dtype=jnp.int32)
    lag_index = first_lag + jnp.arange(lag_count, dtype=jnp.int32) - LMAX
    turn_count = jnp.mod(frequency[:, None] * lag_index[None, :], NFFT)
    angle_rad = turn_count.astype(jnp.float32) * (2.0 * jnp.pi / NFFT)
    cosine = jnp.cos(angle_rad)
    sine_part = jnp.sin(angle_rad)
    upper_half = jnp.concatenate([cosine, sine_part], axis=1)
    lower_half = jnp.concatenate([-sine_part, cosine], axis=1)
    return jnp.concatenate([upper_half, lower_half], axis=0).astype(jnp.bfloat16)


def correlate_block(cross_rows, first_lag, lag_count, windows):
    analytic = jnp.dot(
        cross_rows, lag_table(first_lag, lag_count), preferred_element_type=jnp.float32
    )
    analytic = analytic * (1.0 / jnp.sqrt(jnp.float32(F)))
    real_part = analytic[:, :lag_count]
    imag_part = analytic[:, lag_count:]
    magnitude = jnp.maximum(jnp.sqrt(real_part * real_part + imag_part * imag_part), phase_floor)
    terms = jnp.stack([real_part, real_part / magnitude, imag_part / magnitude], axis=1)
    return terms.reshape(-1, windows, 3, lag_count).sum(axis=1)


def weigh_stack(totals, counts, windows):
    traces = jnp.maximum(counts, 1.0) * windows
    linear = totals[..., 0, :]
    power = totals[..., 1, :] * totals[..., 1, :] + totals[..., 2, :] * totals[..., 2, :]
    return linear / jnp.sqrt(traces)[..., None] * power / traces[..., None]


def gather_rows(partial_value, slot_rows, chan_count):
    is_live = slot_rows >= 0
    safe_rows = jnp.maximum(slot_rows, 0)
    picked = jax.vmap(lambda block_rows, chosen: block_rows[chosen])(partial_value, safe_rows)
    picked = picked * is_live[..., None, None].astype(jnp.float32)
    step_count = slot_rows.shape[0]
    slot_count = NBINS * MOST // chan_count
    buffer = picked.reshape(step_count, chan_count, slot_count, 3, partial_value.shape[-1])
    live_mask = is_live.astype(jnp.float32).reshape(step_count, chan_count, slot_count)
    return (buffer, live_mask)


def fold_slots(received, live_mask):
    step_count, chan_count, slot_count = live_mask.shape
    bin_count = slot_count // MOST
    totals = received.reshape(step_count, chan_count, bin_count, MOST, 3, received.shape[-1]).sum(
        axis=(1, 3)
    )
    counts = live_mask.reshape(step_count, chan_count, bin_count, MOST).sum(axis=(1, 3))
    return (totals, counts)


def shards(spectra, sources, bin_rows):
    chan_dev = spectra.shape[0]
    win_dev = spectra.shape[1]
    chan_count = lax.axis_size("chan")
    windows = win_dev * lax.axis_size("win")
    step_count = sources.shape[0]
    white = whiten(spectra)
    owners = sources // chan_dev
    local_rows = sources % chan_dev
    gathered = []
    for step_index in range(step_count):
        own_row = lax.dynamic_index_in_dim(white, local_rows[step_index], 0, keepdims=False)
        gathered.append(broadcast(own_row, "chan", owners[step_index]))
    source = jnp.stack(gathered)
    cross_rows = cross_spectra(white[None], source[:, None]).reshape(-1, 2 * F)
    block_len = min(256, LAGS)
    block_count = LAGS // block_len

    def one_block(block):
        return correlate_block(cross_rows, block * block_len, block_len, win_dev)

    pieces = lax.map(one_block, jnp.arange(block_count, dtype=jnp.int32))
    pieces = pieces.reshape(block_count, step_count, chan_dev, 3, block_len)
    partial_value = jnp.transpose(pieces, (1, 2, 3, 0, 4)).reshape(step_count, chan_dev, 3, LAGS)
    slot_rows = bin_rows[:, 0]
    buffer, live_mask = gather_rows(partial_value, slot_rows, chan_count)
    received, live_got = (
        lax.all_to_all(buffer, "chan", split_axis=1, concat_axis=1, tiled=True),
        lax.all_to_all(live_mask, "chan", split_axis=1, concat_axis=1, tiled=True),
    )
    totals, counts = fold_slots(received, live_got)
    totals = lax.psum_scatter(totals, "win", scatter_dimension=3, tiled=True)
    return weigh_stack(totals, counts, windows)


def solution(mesh):
    in_specs = (P("chan", "win", None, None), P(), P(None, "chan", None, None))
    out_specs = P(None, "chan", "win")
    return jax.shard_map(shards, mesh=mesh, in_specs=in_specs, out_specs=out_specs, check_vma=False)
```

profile of v0, /device:TPU:1, one launch (start us, length us, event | category | flops | bytes accessed | tf_op | source)
XLA Modules:
  0.0 756.9 jit_solution(268665359414033061)
XLA Ops:
  21.3 4.2 fusion.30
  29.9 81.5 %all-reduce.3.cloned.1.call-done = (bf16[1,4,2,1024]{3,0,1,2:T(2,128)(2,1)}, bf16[1,4,2,1024]{3,0,1,2:T(2,128)(2,1)}, bf16[1,4,2,1024]{3,0,1,2:T(2,128)(2,1)}, bf16[1,4,2,1024]{3,0,1,2:T(2,128)(2,1)}) async-done(((bf16[1,4,2,1024]{3,0,1,2:T(2,128)(2,1)}, bf16[1,4,2,1024]{3,0,1,2:T(2,128)(2,1)}, bf16[1,4,2,1024]{3,0,1,2:T(2,128)(2,1)}, bf16[1,4,2,1024]{3,0,1,2:T(2,128)(2,1)}), ...) | async-done | bytes 65552 | tf_op jit(solution)/shard_map/psum | solution.py:22
  119.0 3.4 pad_maximum_fusion
  122.4 227.0 %while.12 = (s32[]{:T(128)}, f32[16,192,3,256]{3,1,2,0:T(8,128)}, s32[16]{0:T(128)S(1)}, bf16[768,2048]{1,0:T(8,128)(2,1)}, s32[]{:T(128)}, /*index=5*/s32[1]{0:T(128)}) while((s32[]{:T(128)}, f32[16,192,3,256]{3,1,2,0:T(8,128)}, s32[16]{0:T(128)S(1)}, bf16[768,2048]{1,0:T(8,128)(2,1)}, s32[]{:T(128)}, /*index=5*/s32[1]{0:T(128)}) %tuple.55), condition=%wide.region_6.7_spmd, body=%wide.region_4.6_spmd.sunk | while | flops 1626916352 | bytes 25373280 | solution.py:124
  123.7 4.7 fusion.55
  128.5 3.7 multiply_bitcast_fusion.2
  137.9 4.7 fusion.55
  142.6 3.7 multiply_bitcast_fusion.2
  152.1 4.7 fusion.55
  156.8 3.7 multiply_bitcast_fusion.2
  166.3 4.7 fusion.55
  171.0 3.7 multiply_bitcast_fusion.2
  180.4 4.7 fusion.55
  185.2 3.7 multiply_bitcast_fusion.2
  194.6 4.7 fusion.55
  199.3 3.7 multiply_bitcast_fusion.2
  208.8 4.7 fusion.55
  213.5 3.7 multiply_bitcast_fusion.2
  222.9 4.7 fusion.55
  227.7 3.7 multiply_bitcast_fusion.2
  237.1 4.7 fusion.55
  241.8 3.7 multiply_bitcast_fusion.2
  251.3 4.7 fusion.55
  256.0 3.7 multiply_bitcast_fusion.2
  265.5 4.7 fusion.55
  270.2 3.7 multiply_bitcast_fusion.2
  279.6 4.7 fusion.55
  284.3 3.7 multiply_bitcast_fusion.2
  293.8 4.7 fusion.55
  298.5 3.7 multiply_bitcast_fusion.2
  307.9 4.7 fusion.55
  312.7 3.7 multiply_bitcast_fusion.2
  322.1 4.7 fusion.55
  326.8 3.7 multiply_bitcast_fusion.2
  336.3 4.7 fusion.55
  341.1 3.7 multiply_bitcast_fusion.2
  349.4 13.8 %copy.118 = f32[16,4,48,3,256]{4,0,2,3,1:T(8,128)} copy(f32[16,4,48,3,256]{4,2,1,3,0:T(8,128)} %bitcast.98) | data formatting | bytes 18874368 | tf_op jit(solution)/shard_map/reshape | solution.py:125
  363.2 11.3 %reshape.190 = f32[4,48,3,4096]{3,1,2,0:T(8,128)} reshape(f32[4,48,3,16,256]{4,3,1,2,0:T(8,128)} %bitcast.96) | data formatting | bytes 18874368 | tf_op jit(solution)/shard_map/reshape | solution.py:126
  374.5 14.8 %copy.82 = f32[4,48,3,4096]{3,2,1,0:T(4,128)} copy(f32[4,48,3,4096]{3,1,2,0:T(8,128)} %reshape.190) | data formatting | bytes 18874368 | tf_op jit(solution)/shard_map/reshape | solution.py:126
  389.3 31.4 %gather_fusion = f32[384,3,4096]{2,1,0:T(4,128)} fusion(f32[4,48,3,4096]{3,2,1,0:T(4,128)} %copy.82, s32[384]{0:T(512)S(1)} %reshape.200), kind=kCustom, calls=%fused_computation | custom fusion | bytes 37751808 | tf_op jit(solution)/shard_map/vmap()/gather | solution.py:84
  420.7 12.7 %copy_multiply_fusion = f32[4,16,6,3,4096]{4,2,1,0,3:T(8,128)S(1)} fusion(f32[4,16,6,3,4096]{4,3,2,1,0:T(4,128)} %bitcast.95, f32[4,16,6]{2,1,0:T(8,128)S(1)} %reshape.199), kind=kLoop, calls=%fused_computation.30 | loop fusion | flops 4718592 | bytes 37750272 | tf_op jit(solution)/shard_map/mul | solution.py:85
  433.5 17.2 %copy.85 = f32[4,16,6,3,4096]{4,0,3,2,1:T(4,128)} copy(f32[4,16,6,3,4096]{4,2,1,0,3:T(8,128)S(1)} %copy_multiply_fusion) | data formatting | bytes 37748736 | tf_op jit(solution)/shard_map/mul | solution.py:85
  450.7 212.2 %all_to_all.10 = f32[4,16,6,3,4096]{4,0,3,2,1:T(4,128)} all-to-all(f32[4,16,6,3,4096]{4,0,3,2,1:T(4,128)} %copy.85), channel_id=1, replica_groups=mesh['chan'=16,'win'=8] {'chan'}, dimensions={1} | all-to-all | bytes 37748736 | tf_op jit(solution)/shard_map/all_to_all | solution.py:130
  662.9 10.5 %reduce_sum.44 = f32[4,6,3,4096]{3,0,2,1:T(4,128)S(1)} reduce(f32[4,16,6,3,4096]{4,0,3,2,1:T(4,128)} %all_to_all.10, f32[]{:T(128)} %constant.115.clone.1), dimensions={1}, to_apply=%region_7.8 | reduce | flops 4423680 | bytes 20054020 | tf_op jit(solution)/shard_map/reduce_sum | solution.py:96
  673.8 16.9 %copy.91 = f32[4,2,3,4096]{1,0,2,3:T(4,128)} copy(f32[4,2,3,4096]{3,0,2,1:T(4,128)S(1)} %reduce_sum.46) | data formatting | bytes 786432
  690.7 18.1 %reshape.213 = f32[4096,24]{1,0:T(8,128)} reshape(f32[4096,3,4,2]{3,2,1,0:T(4,128)} %bitcast.94) | data formatting | bytes 786432
  708.8 11.5 %all_to_all.11 = f32[4,16,6]{2,0,1:T(4,128)S(1)} all-to-all(f32[4,16,6]{2,0,1:T(4,128)S(1)} %copy.89), channel_id=1, replica_groups=mesh['chan'=16,'win'=8] {'chan'}, dimensions={1} | all-to-all | bytes 3072 | tf_op jit(solution)/shard_map/all_to_all | solution.py:131
  720.5 19.5 %reduce-scatter.4.cloned.1.call-done = f32[512,24]{1,0:T(8,128)} async-done(((f32[4096,24]{1,0:T(8,128)}), f32[512,24]{1,0:T(8,128)}) %reduce-scatter.4.cloned.1.call-update) | async-done | bytes 49168
  (233 shorter events, 107.3 us)
Async XLA Ops:
  6.5 104.9 %all-reduce.3.cloned.1.call-start = ((), (), s32[]{:S(2)}) async-start(), calls=%async_computation.4 | async-start | bytes 262144 | tf_op jit(solution)/shard_map/psum | solution.py:22
  21.3 5.7 copy-start.1
  26.4 713.7 %reduce-scatter.4.cloned.1.call-start = ((), (), s32[]{:S(2)}) async-start(), calls=%async_computation.3 | async-start | bytes 2359296
  117.2 1.9 copy-start
Sparse Core Ops, SparseCore 0:
  26.5 84.8 all-reduce.2
  708.9 31.0 reduce-scatter.3
where the time goes:
time: 766 us; the launch traced here: 757 us
  blocking collectives  224 us (29%)
  local copies, waits for them, and re-layouts  191 us (25%)
  other arithmetic  141 us (18%)
  waiting for transfers between devices  101 us (13%)
  matrix products  63.9 us (8%)
  between operations  23.8 us (3%)
  loops' own time  11.6 us (2%)
    all_to_all x1, blocking collectives, shards(): lax.all_to_all(buffer, 'chan', split_axis=1, concat_axis=1, tiled=True)  212 us
    psum x1, waiting for transfers between devices, broadcast(): return lax.psum(block, axis)  81.5 us
    another operation x17, other arithmetic  78.3 us
    dot_general x16, matrix products, correlate_block(): jnp.dot(cross_rows, lag_table(first_lag, lag_count), preferred_element_ty...  59.6 us
    unnamed x10, local copies, waits for them, and re-layouts  42.2 us
    gather x3, local copies, waits for them, and re-layouts, gather_rows(): block_rows[chosen]  31.7 us
    reduce_sum x16, other arithmetic, correlate_block(): return terms.reshape(-1, windows, 3, lag_count).sum(axis=1)  26.3 us
    reshape x2, local copies, waits for them, and re-layouts, shards(): jnp.transpose(pieces, (1, 2, 3, 0, 4))  26.1 us
  transfers between devices with their start and end apart: 2, of which 2 were waited for; matrix products, arithmetic and copies ran while one was open for 0% of the time, Pallas kernels for 0%

commit v1 on v0

v1 whole, which is shorter than its diff:
```python
import jax
import jax.numpy as jnp
import numpy as np
from jax import lax
from jax.experimental import pallas as pl
from jax.experimental.pallas import tpu as pltpu
from jax.sharding import Mesh, PartitionSpec as P

F = 1024
F0 = 32
NFFT = 8192
HW = 32
NBINS = 32
EPS = 1e-06
FLOOR = 0.1
BLOCK = 512
HALF = 256
PAIRS = 4
bf16 = jnp.bfloat16
f32 = jnp.float32


def lag_tables():
    frequency = F0 + np.arange(F, dtype=np.int64)

    def pair(lags):
        angle = (frequency[:, None] * lags[None, :]) % NFFT * (2.0 * np.pi / NFFT)
        return np.concatenate([np.cos(angle), np.sin(angle)], axis=1).astype(bf16)

    blocks = [
        np.concatenate(
            [pair(b * BLOCK + h * HALF + np.arange(HALF)) for h in range(2)], axis=1
        )
        for b in range(PAIRS)
    ]
    return np.stack(blocks), pair(np.full((128,), 2048))


def smooth_amplitude(re, im):
    amp = jnp.sqrt(re * re + im * im)
    wide = F + 128
    padded = jnp.concatenate([amp, jnp.zeros((amp.shape[0], 128), f32)], axis=1)
    total = padded
    for k in (1, 2, 4, 8, 16, 32):
        total = total + pltpu.roll(total, k, 1)
    total = pltpu.roll(total, wide - HW, 1) + pltpu.roll(padded, HW, 1)
    return total[:, :F] * (1.0 / (2 * HW + 1)) + EPS


def whiten_kernel(x_ref, o_ref):
    for g in range(3):
        rows = slice(16 * g, 16 * g + 16)
        re = x_ref[0, 0, rows, :].astype(f32)
        im = x_ref[1, 0, rows, :].astype(f32)
        inv = 1.0 / smooth_amplitude(re, im)
        o_ref[0, 0, rows, :] = (re * inv).astype(bf16)
        o_ref[1, 0, rows, :] = (im * inv).astype(bf16)


def whiten(x):
    spec = pl.BlockSpec((2, 1, 48, F), lambda w: (0, w, 0, 0))
    return pl.pallas_call(
        whiten_kernel,
        grid=(x.shape[1],),
        in_specs=[spec],
        out_specs=spec,
        out_shape=jax.ShapeDtypeStruct(x.shape, bf16),
        name="whiten",
    )(x)


def stack_kernel(
    mine_ref, other_ref, src_ref, table_ref, edge_table_ref, member_ref, out_ref,
    src_sc, cross_sc, prod_sc, edge_prod_sc, minus_sc, edge_sc, sums_sc,
):
    step_id = pl.program_id(0)
    block = PAIRS - 1 - step_id
    floor2 = (FLOOR * 32.0) ** 2

    def unit(re, im):
        inv = lax.rsqrt(jnp.maximum(re * re + im * im, floor2))
        return re * inv, im * inv

    @pl.when(step_id == 0)
    def _():
        re = src_ref[0:16, :].astype(f32)
        im = src_ref[16:32, :].astype(f32)
        inv = 1.0 / smooth_amplitude(re, im)
        src_sc[0] = (re * inv).astype(bf16).astype(f32)
        src_sc[1] = (im * inv).astype(bf16).astype(f32)
        for s in range(2):
            for w in range(8):
                half, wl = divmod(w, 4)
                row = half * 8 + s * 4 + wl
                ref = other_ref if half else mine_ref
                for g in range(3):
                    rows = slice(16 * g, 16 * g + 16)
                    sr = jnp.broadcast_to(src_sc[0, row : row + 1, :], (16, F))
                    si = jnp.broadcast_to(src_sc[1, row : row + 1, :], (16, F))
                    wr = ref[0, wl, rows, :].astype(f32)
                    wi = ref[1, wl, rows, :].astype(f32)
                    at = w * 48 + 16 * g
                    cross_sc[s, at : at + 16, :] = (wr * sr + wi * si).astype(bf16)
                    cross_sc[s, 384 + at : 384 + at + 16, :] = (wi * sr - wr * si).astype(bf16)
        for s in range(2):
            edge_prod_sc[...] = jnp.dot(cross_sc[s], edge_table_ref[...], preferred_element_type=f32)
            for g in range(6):
                lin = jnp.zeros((8, 128), f32)
                pr, pi = lin, lin
                for w in range(8):
                    at = w * 48 + 8 * g
                    a = edge_prod_sc[at : at + 8, :128]
                    d = edge_prod_sc[at : at + 8, 128:]
                    c = edge_prod_sc[384 + at : 384 + at + 8, :128]
                    b = edge_prod_sc[384 + at : 384 + at + 8, 128:]
                    lin = lin + (a + b)
                    ur, ui = unit(a + b, c - d)
                    pr, pi = pr + ur, pi + ui
                for k, value in enumerate((lin, pr, pi)):
                    edge_sc[k, s, 8 * g : 8 * g + 8, :] = value

    def product(i):
        h, s = divmod(i, 2)
        prod_sc[i % 2] = jnp.dot(
            cross_sc[s], table_ref[0, :, h * 512 : h * 512 + 512], preferred_element_type=f32
        )

    def epilogue(i):
        h, s = divmod(i, 2)
        slot = i % 2
        for g in range(3):
            for t in range(2):
                zero = jnp.zeros((16, 128), f32)
                sa, sb, pr, pi, mr, mi = (zero,) * 6
                for w in range(8):
                    at = w * 48 + 16 * g
                    lo = slice(128 * t, 128 * t + 128)
                    hi = slice(256 + 128 * t, 256 + 128 * t + 128)
                    a = prod_sc[slot, at : at + 16, lo]
                    d = prod_sc[slot, at : at + 16, hi]
                    c = prod_sc[slot, 384 + at : 384 + at + 16, lo]
                    b = prod_sc[slot, 384 + at : 384 + at + 16, hi]
                    sa, sb = sa + a, sb + b
                    ur, ui = unit(a - b, c + d)
                    pr, pi = pr + ur, pi + ui
                    ur, ui = unit(a + b, c - d)
                    mr, mi = mr + ur, mi + ui
                at = h * 96 + s * 48 + 16 * g
                for k, value in enumerate((sa - sb, pr, pi)):
                    sums_sc[0, k, at : at + 16, 128 * t : 128 * t + 128] = value.astype(bf16)
                for k, value in enumerate((sa + sb, mr, mi)):
                    lo = 256 * h + 128 * t
                    minus_sc[k, s, 16 * g : 16 * g + 16, lo : lo + 128] = value

    product(0)
    for i in range(1, 4):
        product(i)
        epilogue(i - 1)
    epilogue(3)
    last = lax.broadcasted_iota(jnp.int32, (48, 128), 1) == 127
    for k in range(3):
        for s in range(2):
            moved = pltpu.roll(minus_sc[k, s], BLOCK - 1, 1)
            tail = moved[:, 384:]
            new_tail = jnp.where(last, edge_sc[k, s], tail)
            edge_sc[k, s] = tail
            at = s * 48
            sums_sc[1, k, at : at + 48, :] = moved[:, :256].astype(bf16)
            sums_sc[1, k, 96 + at : 96 + at + 48, :128] = moved[:, 256:384].astype(bf16)
            sums_sc[1, k, 96 + at : 96 + at + 48, 128:] = new_tail.astype(bf16)
    for sign in range(2):
        win = PAIRS - 1 - block if sign else PAIRS + block
        for k in range(3):
            binned = jnp.dot(member_ref[...], sums_sc[sign, k], preferred_element_type=f32)
            out_ref[:, win, k] = binned.reshape(16, 8, HALF).astype(bf16)


def stack_partial(mine, other, src, member):
    table, edge_table = lag_tables()
    whole = lambda *shape: pl.BlockSpec(shape, lambda b: (0,) * len(shape), pipeline_mode=pl.Buffered(1))
    return pl.pallas_call(
        stack_kernel,
        grid=(PAIRS,),
        in_specs=[
            whole(2, 4, 48, F),
            whole(2, 4, 48, F),
            whole(32, F),
            pl.BlockSpec((1, F, 1024), lambda b: (PAIRS - 1 - b, 0, 0)),
            whole(F, 256),
            whole(128, 192),
        ],
        out_specs=whole(16, 8, 3, 8, HALF),
        out_shape=jax.ShapeDtypeStruct((16, 8, 3, 8, HALF), bf16),
        scratch_shapes=[
            pltpu.VMEM((2, 16, F), f32),
            pltpu.VMEM((2, 768, F), bf16),
            pltpu.VMEM((2, 768, 512), f32),
            pltpu.VMEM((768, 256), f32),
            pltpu.VMEM((3, 2, 48, BLOCK), f32),
            pltpu.VMEM((3, 2, 48, 128), f32),
            pltpu.VMEM((2, 3, 192, HALF), bf16),
        ],
        compiler_params=pltpu.CompilerParams(vmem_limit_bytes=48 << 20),
        name="stack",
    )(mine, other, src, jnp.asarray(table), jnp.asarray(edge_table), member)


def shift(count):
    return [(i, (i + count) % 4) for i in range(4)]


def shards(spectra, sources, bin_rows):
    y, z, x, c = (lax.axis_index(a) for a in ("y", "z", "x", "c"))
    chan = y * 4 + z
    chan_dev, win_dev = spectra.shape[:2]
    windows = win_dev * 8
    swap = [(0, 1), (1, 0)]
    slot_rows = bin_rows[:, 0]

    owners, rows = sources // chan_dev, sources % chan_dev
    picked = [
        jnp.where(owners[s] == chan, lax.dynamic_index_in_dim(spectra, rows[s], 0, keepdims=False), 0)
        for s in range(4)
    ]
    counts = jnp.sum((slot_rows >= 0).astype(f32), axis=2).astype(bf16)
    counts = jnp.pad(counts.reshape(1, 128), ((0, 7), (0, F - 128)))
    sent = jnp.concatenate([jnp.stack(picked).reshape(32, F), counts], axis=0)
    for axis in ("z", "y"):
        got = [lax.ppermute(sent, axis, shift(k)) for k in (1, 3, 2)]
        sent = (sent + got[0]) + (got[1] + got[2])
    counts = sent[32, :128].astype(f32).reshape(4, NBINS)
    src = sent[:32].reshape(2, 2, 4, 2, F)
    src_mine = lax.dynamic_index_in_dim(src, c, 0, keepdims=False)
    src_other = lax.ppermute(lax.dynamic_index_in_dim(src, 1 - c, 0, keepdims=False), "c", swap)
    src = jnp.transpose(jnp.stack([src_mine, src_other]), (3, 0, 1, 2, 4)).reshape(32, F)

    mine = whiten(jnp.transpose(spectra, (2, 1, 0, 3)))
    other = lax.ppermute(mine, "c", swap)

    own_rows = lax.dynamic_slice_in_dim(slot_rows, 2 * c, 2, 0)
    member = jnp.any(own_rows[..., None] == jnp.arange(chan_dev), axis=2).reshape(2, 16, 2, chan_dev)
    member = jnp.transpose(member, (1, 0, 2, 3)).astype(bf16)
    eye = jnp.eye(2, dtype=bf16)
    member = (
        member[:, None, :, :, None, None, :]
        * eye[None, :, None, None, :, None, None]
        * eye[None, None, :, None, None, :, None]
    ).reshape(128, 4 * chan_dev)

    partial = stack_partial(mine, other, src, member)
    received = lax.all_to_all(partial.reshape(64, 6, 8, HALF), ("y", "z", "x"), 0, 0, tiled=True)
    totals = jnp.sum(received.astype(f32), axis=0).reshape(2, 3, 2, 2, 2, HALF)
    counts = lax.dynamic_slice(counts, (2 * c, 2 * chan), (2, 2))
    traces = (jnp.maximum(counts, 1.0) * windows)[None, None, :, :, None]
    linear, pr, pi = totals[:, 0] * (1.0 / 32.0), totals[:, 1], totals[:, 2]
    stacked = linear / jnp.sqrt(traces) * (pr * pr + pi * pi) / traces
    keep = lax.dynamic_index_in_dim(stacked, c, 0, keepdims=False)
    send = lax.dynamic_index_in_dim(stacked, 1 - c, 0, keepdims=False)
    got = lax.ppermute(send, "c", swap)
    both = jnp.where(c == 0, jnp.stack([keep, got]), jnp.stack([got, keep]))
    out = jnp.transpose(both, (0, 2, 3, 1, 4)).reshape(4, 2, BLOCK)
    return jnp.where(x < 2, out[..., ::-1], out)


def solution(mesh):
    fine = Mesh(mesh.devices.reshape(4, 4, 4, 2), ("y", "z", "x", "c"))
    chan, win = ("y", "z"), ("x", "c")
    in_specs = (P(chan, win, None, None), P(), P(None, chan, None, None))
    return jax.shard_map(
        shards, mesh=fine, in_specs=in_specs, out_specs=P(None, chan, win), check_vma=False
    )
```

time: 766 us -> 98.2 us (0.13); the launches traced: 757 us -> 97.7 us
  blocking collectives: 224 us -> 0 us
  local copies, waits for them, and re-layouts: 191 us -> 4.07 us
  other arithmetic: 141 us -> 3.9 us
  waiting for transfers between devices: 101 us -> 28.6 us
  matrix products: 63.9 us -> 0 us
  Pallas kernels: 0 us -> 27.9 us
  starting transfers between devices: 0.57 us -> 22.7 us
  between operations: 23.8 us -> 10.5 us
  loops' own time: 11.6 us -> 0 us
    all_to_all x2 -> x0, blocking collectives: 224 us -> none  [the longest x1 212 us: shards(): lax.all_to_all(buffer, 'chan', split_axis=1, concat_axis=1, tiled=True)]
    psum x1 -> x0, waiting for transfers between devices: 81.5 us -> none  [broadcast(): return lax.psum(block, axis)]
    another operation x17 -> x1, other arithmetic: 78.3 us -> 0.11 us  [shards(): sent = jnp.concatenate([jnp.stack(picked).reshape(32, F), counts], axis=0)]
    dot_general x17 -> x0, matrix products: 63.9 us -> none  [the longest x16 59.6 us: correlate_block(): jnp.dot(cross_rows, lag_table(first_lag, lag_count), preferred_element_ty...]
    reshape x3 -> x5, local copies, waits for them, and re-layouts: 39.9 us -> 0.13 us  [the longest x1 0.03 us: shards(): sent = jnp.concatenate([jnp.stack(picked).reshape(32, F), counts], axis=0)]
    unnamed x10 -> x8, local copies, waits for them, and re-layouts: 42.2 us -> 2.48 us
    reduce_sum x20 -> x2, other arithmetic: 37.3 us -> 0.96 us  [the longest x1 0.72 us: shards(): counts = jnp.sum((slot_rows >= 0).astype(f32), axis=2).astype(bf16)]
    gather x3 -> x0, local copies, waits for them, and re-layouts: 31.7 us -> none  [gather_rows(): block_rows[chosen]]
  transfers between devices with their start and end apart: 2 -> 10, of which waited for: 2 -> 6; matrix products, arithmetic and copies ran while one was open for 0% -> 4% of each run, Pallas kernels for 0% -> 5%
where the time goes in v1:
time: 98.2 us; the launch traced here: 97.7 us
  waiting for transfers between devices  28.6 us (29%)
  Pallas kernels  27.9 us (28%)
  starting transfers between devices  22.7 us (23%)
  between operations  10.5 us (11%)
  local copies, waits for them, and re-layouts  4.07 us (4%)
  other arithmetic  3.9 us (4%)
    all_to_all x1, waiting for transfers between devices, shards(): lax.all_to_all(partial.reshape(64, 6, 8, HALF), ('y', 'z', 'x'), 0, 0, ti...  23.5 us
    pallas_call x1, Pallas kernels, stack_partial(): pl.pallas_call(stack_kernel, grid=(PAIRS,), in_specs=[whole(2, 4, 48, F),...  22.8 us
    ppermute x6, starting transfers between devices, shards(): got = [lax.ppermute(sent, axis, shift(k)) for k in (1, 3, 2)]  9.81 us
    all_to_all x1, starting transfers between devices, shards(): lax.all_to_all(partial.reshape(64, 6, 8, HALF), ('y', 'z', 'x'), 0, 0, ti...  7.62 us
    pallas_call x1, Pallas kernels, whiten(): pl.pallas_call(whiten_kernel, grid=(x.shape[1],), in_specs=[spec], out_sp...  5.09 us
    ppermute x6, waiting for transfers between devices, shards(): got = [lax.ppermute(sent, axis, shift(k)) for k in (1, 3, 2)]  3.7 us
    unnamed x8, local copies, waits for them, and re-layouts  2.48 us
    ppermute x1, starting transfers between devices, shards(): got = lax.ppermute(send, 'c', swap)  1.98 us
  transfers between devices with their start and end apart: 10, of which 6 were waited for; matrix products, arithmetic and copies ran while one was open for 4% of the time, Pallas kernels for 5%

profile of v1, /device:TPU:1, one launch (start us, length us, event | category | flops | bytes accessed | tf_op | source)
XLA Modules:
  0.0 97.7 jit_solution(7887321960112390124)
XLA Ops:
  0.0 0.7 and_select_fusion
  0.7 0.7 fusion.12
  6.5 0.7 fusion.9
  7.2 0.1 convert_element_type.58
  12.4 0.8 broadcast_select_fusion.3
  13.2 0.1 pad_maximum_fusion
  13.4 0.0 copy-start.2
  13.4 4.7 %collective-permute-start.2 = (bf16[40,1024]{1,0:T(8,128)(2,1)S(1)}, bf16[40,1024]{1,0:T(8,128)(2,1)S(1)}, u32[]{:S(2)}, u32[]{:S(2)}) collective-permute-start(bf16[40,1024]{1,0:T(8,128)(2,1)S(1)} %fusion.2), channel_id=1, source_target_pairs={{0,24},{8,0},{16,8},{24,16},{1,25},{9,1},{17,9},{25,17},{2,26},{10... | collective-permute-start | bytes 245768 | tf_op jit(solution)/shard_map/ppermute | solution.py:229
  18.1 0.0 collective-permute-start.3
  18.1 0.7 collective-permute-start.1
  18.8 2.5 %copy.39 = bf16[48,4,2,1024]{3,0,1,2:T(8,128)(2,1)} copy(bf16[48,4,2,1024]{3,2,1,0:T(2,128)(2,1)} %param.5) | data formatting | bytes 1572864 | tf_op args[0]
  21.2 0.0 copy-start.1
  21.2 5.1 %whiten.1.mine_ref = bf16[2,4,48,1024]{3,2,1,0:T(8,128)(2,1)} custom-call(bf16[2,4,48,1024]{3,2,1,0:T(8,128)(2,1)} %bitcast.54), custom_call_target="tpu_custom_call" | custom-call | tf_op jit(solution)/shard_map/whiten/pallas_call | solution.py:62
  26.3 0.0 copy-start
  26.3 1.5 %collective-permute-start = (bf16[2,4,48,1024]{3,2,1,0:T(8,128)(2,1)}, bf16[2,4,48,1024]{3,2,1,0:T(8,128)(2,1)S(1)}, u32[]{:S(2)}, u32[]{:S(2)}) collective-permute-start(bf16[2,4,48,1024]{3,2,1,0:T(8,128)(2,1)} %whiten.1.mine_ref), channel_id=1, source_target_pairs={{0,1},{1,0},{2,3},{3,2},{4,5},{5,4},{6,7},{7,6},{8,9},{9,8},{10,11... | collective-permute-start | bytes 2359304 | tf_op jit(solution)/shard_map/ppermute | solution.py:238
  27.8 0.0 copy-done.2
  27.8 0.1 fusion.1
  28.0 0.0 collective-permute-done.2
  28.0 0.0 collective-permute-done.3
  28.0 0.0 collective-permute-done.1
  28.1 3.0 %collective-permute-start.6 = (bf16[40,1024]{1,0:T(8,128)(2,1)S(1)}, bf16[40,1024]{1,0:T(8,128)(2,1)S(1)}, u32[]{:S(2)}, u32[]{:S(2)}) collective-permute-start(bf16[40,1024]{1,0:T(8,128)(2,1)S(1)} %add_add_fusion.1), channel_id=1, source_target_pairs={{0,64},{32,96},{64,0},{96,32},{1,65},{33,97},{65,1},{97,33},{2,66}... | collective-permute-start | bytes 245768 | tf_op jit(solution)/shard_map/ppermute | solution.py:229
  31.0 0.8 collective-permute-start.5
  31.8 0.7 collective-permute-start.4
  32.5 0.1 broadcast_multiply_fusion.1
  32.6 1.1 %collective-permute-done.6 = bf16[40,1024]{1,0:T(8,128)(2,1)S(1)} collective-permute-done((bf16[40,1024]{1,0:T(8,128)(2,1)S(1)}, bf16[40,1024]{1,0:T(8,128)(2,1)S(1)}, u32[]{:S(2)}, u32[]{:S(2)}) %collective-permute-start.6) | collective-permute-done | bytes 81952 | tf_op jit(solution)/shard_map/ppermute | solution.py:229
  33.7 2.1 %collective-permute-done.5 = bf16[40,1024]{1,0:T(8,128)(2,1)S(1)} collective-permute-done((bf16[40,1024]{1,0:T(8,128)(2,1)S(1)}, bf16[40,1024]{1,0:T(8,128)(2,1)S(1)}, u32[]{:S(2)}, u32[]{:S(2)}) %collective-permute-start.5) | collective-permute-done | bytes 81952 | tf_op jit(solution)/shard_map/ppermute | solution.py:229
  35.8 0.5 collective-permute-done.4
  36.4 0.1 constant_dynamic-slice_fusion.3
  36.5 1.8 %collective-permute-start.7 = (bf16[2,4,2,1024]{3,1,0,2:T(4,128)(2,1)S(1)}, bf16[2,4,2,1024]{3,1,0,2:T(4,128)(2,1)S(1)}, u32[]{:S(2)}, u32[]{:S(2)}) collective-permute-start(bf16[2,4,2,1024]{3,1,0,2:T(4,128)(2,1)S(1)} %bitcast.58), channel_id=1, source_target_pairs={{0,1},{1,0},{2,3},{3,2},{4,5},{5,4},{6,7},{7,6},{8,9},{9,8},{10,11... | collective-permute-start | bytes 98312 | tf_op jit(solution)/shard_map/ppermute | solution.py:234
  38.3 0.2 broadcast_multiply_fusion
  38.5 0.1 mul.76.member_ref
  38.6 0.5 collective-permute-done.7
  39.2 0.0 collective-permute-done.other_ref
  39.2 0.0 copy-done.1
  39.3 0.0 copy-done
  39.3 22.8 %stack.33 = bf16[16,8,3,8,256]{4,3,2,1,0:T(8,128)(2,1)} custom-call(bf16[2,4,48,1024]{3,2,1,0:T(8,128)(2,1)S(1)} %copy-done, bf16[2,4,48,1024]{3,2,1,0:T(8,128)(2,1)S(1)} %collective-permute-done.other_ref, bf16[32,1024]{1,0:T(8,128)(2,1)S(1)} %reshape.81.src_ref, bf16[4,1024,1024]{2,1,0:T(8,128)(2,1)} %constant.85.clone.table_ref, ...), custom_call_target="tpu_custom_call" | custom-call | tf_op jit(solution)/shard_map/stack/pallas_call | solution.py:181
  62.1 7.6 %all-to-all-start = ((bf16[64,6,8,256]{3,2,1,0:T(8,128)(2,1)}), bf16[64,6,8,256]{3,2,1,0:T(8,128)(2,1)S(1)}, u32[]{:S(2)}, u32[]{:S(2)}) async-start(bf16[64,6,8,256]{3,2,1,0:T(8,128)(2,1)} %bitcast.15), calls=%async_computation | async-start | bytes 3145728 | tf_op jit(solution)/shard_map/all_to_all | solution.py:251
  69.7 0.1 reshape.85
  69.8 0.1 fusion.11
  69.9 23.5 %all-to-all-done = bf16[64,6,8,256]{3,2,1,0:T(8,128)(2,1)S(1)} async-done(((bf16[64,6,8,256]{3,2,1,0:T(8,128)(2,1)}), bf16[64,6,8,256]{3,2,1,0:T(8,128)(2,1)S(1)}, u32[]{:S(2)}, u32[]{:S(2)}) %all-to-all-start) | async-done | bytes 1572896 | tf_op jit(solution)/shard_map/all_to_all | solution.py:251
  93.4 0.2 convert_reduce_fusion
  93.7 0.1 fusion.8
  93.8 2.0 %collective-permute-start.8 = (f32[2,2,2,256]{3,2,1,0:T(2,128)S(1)}, f32[2,2,2,256]{3,2,1,0:T(2,128)S(1)}, u32[]{:S(2)}, u32[]{:S(2)}) collective-permute-start(f32[2,2,2,256]{3,2,1,0:T(2,128)S(1)} %get-tuple-element.14), channel_id=1, source_target_pairs={{0,1},{1,0},{2,3},{3,2},{4,5},{5,4},{6,7},{7,6},{8,9},{9,8},{10,11... | collective-permute-start | bytes 24584 | tf_op jit(solution)/shard_map/ppermute | solution.py:259
  95.8 0.8 collective-permute-done.8
  96.7 0.4 rev.3
  97.0 0.6 broadcast_select_fusion.4
  (21 shorter events, 0.4 us)
Async XLA Ops:
  13.4 14.4 %copy-start.2 = (s32[4,1,32,3]{2,1,3,0:T(1,128)S(1)}, s32[4,1,32,3]{2,1,3,0:T(1,128)}, u32[]{:S(2)}) copy-start(s32[4,1,32,3]{2,1,3,0:T(1,128)} %param.7) | copy-start | bytes 4612
  13.4 14.6 %collective-permute-start.2 = (bf16[40,1024]{1,0:T(8,128)(2,1)S(1)}, bf16[40,1024]{1,0:T(8,128)(2,1)S(1)}, u32[]{:S(2)}, u32[]{:S(2)}) collective-permute-start(bf16[40,1024]{1,0:T(8,128)(2,1)S(1)} %fusion.2), channel_id=1, source_target_pairs={{0,24},{8,0},{16,8},{24,16},{1,25},{9,1},{17,9},{25,17},{2,26},{10... | collective-permute-start | bytes 245768 | tf_op jit(solution)/shard_map/ppermute | solution.py:229
  18.1 9.9 %collective-permute-start.3 = (bf16[40,1024]{1,0:T(8,128)(2,1)S(1)}, bf16[40,1024]{1,0:T(8,128)(2,1)S(1)}, u32[]{:S(2)}, u32[]{:S(2)}) collective-permute-start(bf16[40,1024]{1,0:T(8,128)(2,1)S(1)} %fusion.2), channel_id=1, source_target_pairs={{0,16},{8,24},{16,0},{24,8},{1,17},{9,25},{17,1},{25,9},{2,18},{10... | collective-permute-start | bytes 245768 | tf_op jit(solution)/shard_map/ppermute | solution.py:229
  18.1 9.9 %collective-permute-start.1 = (bf16[40,1024]{1,0:T(8,128)(2,1)S(1)}, bf16[40,1024]{1,0:T(8,128)(2,1)S(1)}, u32[]{:S(2)}, u32[]{:S(2)}) collective-permute-start(bf16[40,1024]{1,0:T(8,128)(2,1)S(1)} %fusion.2), channel_id=1, source_target_pairs={{0,8},{8,16},{16,24},{24,0},{1,9},{9,17},{17,25},{25,1},{2,10},{10... | collective-permute-start | bytes 245768 | tf_op jit(solution)/shard_map/ppermute | solution.py:229
  21.2 18.0 %copy-start.1 = (bf16[1024,256]{1,0:T(8,128)(2,1)S(1)}, bf16[1024,256]{1,0:T(8,128)(2,1)}, u32[]{:S(2)}) copy-start(bf16[1024,256]{1,0:T(8,128)(2,1)} %constant.86.clone.edge_table_ref) | copy-start | bytes 1572868
  26.3 13.0 %copy-start = (bf16[2,4,48,1024]{3,2,1,0:T(8,128)(2,1)S(1)}, bf16[2,4,48,1024]{3,2,1,0:T(8,128)(2,1)}, u32[]{:S(2)}) copy-start(bf16[2,4,48,1024]{3,2,1,0:T(8,128)(2,1)} %whiten.1.mine_ref) | copy-start | bytes 2359300
  26.3 12.9 %collective-permute-start = (bf16[2,4,48,1024]{3,2,1,0:T(8,128)(2,1)}, bf16[2,4,48,1024]{3,2,1,0:T(8,128)(2,1)S(1)}, u32[]{:S(2)}, u32[]{:S(2)}) collective-permute-start(bf16[2,4,48,1024]{3,2,1,0:T(8,128)(2,1)} %whiten.1.mine_ref), channel_id=1, source_target_pairs={{0,1},{1,0},{2,3},{3,2},{4,5},{5,4},{6,7},{7,6},{8,9},{9,8},{10,11... | collective-permute-start | bytes 2359304 | tf_op jit(solution)/shard_map/ppermute | solution.py:238
  28.1 5.6 %collective-permute-start.6 = (bf16[40,1024]{1,0:T(8,128)(2,1)S(1)}, bf16[40,1024]{1,0:T(8,128)(2,1)S(1)}, u32[]{:S(2)}, u32[]{:S(2)}) collective-permute-start(bf16[40,1024]{1,0:T(8,128)(2,1)S(1)} %add_add_fusion.1), channel_id=1, source_target_pairs={{0,64},{32,96},{64,0},{96,32},{1,65},{33,97},{65,1},{97,33},{2,66}... | collective-permute-start | bytes 245768 | tf_op jit(solution)/shard_map/ppermute | solution.py:229
  31.0 4.7 %collective-permute-start.5 = (bf16[40,1024]{1,0:T(8,128)(2,1)S(1)}, bf16[40,1024]{1,0:T(8,128)(2,1)S(1)}, u32[]{:S(2)}, u32[]{:S(2)}) collective-permute-start(bf16[40,1024]{1,0:T(8,128)(2,1)S(1)} %add_add_fusion.1), channel_id=1, source_target_pairs={{0,96},{32,0},{64,32},{96,64},{1,97},{33,1},{65,33},{97,65},{2,98}... | collective-permute-start | bytes 245768 | tf_op jit(solution)/shard_map/ppermute | solution.py:229
  31.8 4.5 %collective-permute-start.4 = (bf16[40,1024]{1,0:T(8,128)(2,1)S(1)}, bf16[40,1024]{1,0:T(8,128)(2,1)S(1)}, u32[]{:S(2)}, u32[]{:S(2)}) collective-permute-start(bf16[40,1024]{1,0:T(8,128)(2,1)S(1)} %add_add_fusion.1), channel_id=1, source_target_pairs={{0,32},{32,64},{64,96},{96,0},{1,33},{33,65},{65,97},{97,1},{2,34}... | collective-permute-start | bytes 245768 | tf_op jit(solution)/shard_map/ppermute | solution.py:229
  36.5 2.7 %collective-permute-start.7 = (bf16[2,4,2,1024]{3,1,0,2:T(4,128)(2,1)S(1)}, bf16[2,4,2,1024]{3,1,0,2:T(4,128)(2,1)S(1)}, u32[]{:S(2)}, u32[]{:S(2)}) collective-permute-start(bf16[2,4,2,1024]{3,1,0,2:T(4,128)(2,1)S(1)} %bitcast.58), channel_id=1, source_target_pairs={{0,1},{1,0},{2,3},{3,2},{4,5},{5,4},{6,7},{7,6},{8,9},{9,8},{10,11... | collective-permute-start | bytes 98312 | tf_op jit(solution)/shard_map/ppermute | solution.py:234
  62.1 31.3 %all-to-all-start = ((bf16[64,6,8,256]{3,2,1,0:T(8,128)(2,1)}), bf16[64,6,8,256]{3,2,1,0:T(8,128)(2,1)S(1)}, u32[]{:S(2)}, u32[]{:S(2)}) async-start(bf16[64,6,8,256]{3,2,1,0:T(8,128)(2,1)} %bitcast.15), calls=%async_computation | async-start | bytes 3145728 | tf_op jit(solution)/shard_map/all_to_all | solution.py:251
  93.8 2.8 %collective-permute-start.8 = (f32[2,2,2,256]{3,2,1,0:T(2,128)S(1)}, f32[2,2,2,256]{3,2,1,0:T(2,128)S(1)}, u32[]{:S(2)}, u32[]{:S(2)}) collective-permute-start(f32[2,2,2,256]{3,2,1,0:T(2,128)S(1)} %get-tuple-element.14), channel_id=1, source_target_pairs={{0,1},{1,0},{2,3},{3,2},{4,5},{5,4},{6,7},{7,6},{8,9},{9,8},{10,11... | collective-permute-start | bytes 24584 | tf_op jit(solution)/shard_map/ppermute | solution.py:259

commit v2 on v1

--- a/solution.py
+++ b/solution.py
@@ -47,6 +47,49 @@
     return total[:, :F] * (1.0 / (2 * HW + 1)) + EPS
 
 
+def pick_kernel(sources_ref, slots_ref, spectra_ref, out_ref, sem):
+    me = lax.axis_index("y") * 4 + lax.axis_index("z")
+    for s in range(4):
+        owner, row = sources_ref[s] // 48, sources_ref[s] % 48
+        copy = pltpu.make_async_copy(spectra_ref.at[row], out_ref.at[s], sem.at[s])
+
+        @pl.when(owner == me)
+        def _(copy=copy):
+            copy.start()
+
+        @pl.when(owner != me)
+        def _(s=s):
+            out_ref[s] = jnp.zeros((4, 2, F), bf16)
+
+    out_ref[4] = jnp.zeros((4, 2, F), bf16)
+    for s in range(4):
+        live = (slots_ref[s] >= 0).astype(f32)
+        count = live[0] + live[1] + live[2]
+        out_ref[4, s, :, :NBINS] = jnp.broadcast_to(count, (2, NBINS)).astype(bf16)
+    for s in range(4):
+        owner, row = sources_ref[s] // 48, sources_ref[s] % 48
+        copy = pltpu.make_async_copy(spectra_ref.at[row], out_ref.at[s], sem.at[s])
+
+        @pl.when(owner == me)
+        def _(copy=copy):
+            copy.wait()
+
+
+def pick(spectra, sources, slots):
+    return pl.pallas_call(
+        pick_kernel,
+        in_specs=[
+            pl.BlockSpec(memory_space=pltpu.SMEM),
+            pl.BlockSpec(memory_space=pltpu.VMEM),
+            pl.BlockSpec(memory_space=pl.ANY),
+        ],
+        out_specs=pl.BlockSpec(memory_space=pltpu.VMEM),
+        out_shape=jax.ShapeDtypeStruct((5, 4, 2, F), bf16),
+        scratch_shapes=[pltpu.SemaphoreType.DMA((4,))],
+        name="pick",
+    )(sources, slots, spectra)
+
+
 def whiten_kernel(x_ref, o_ref):
     for g in range(3):
         rows = slice(16 * g, 16 * g + 16)
@@ -70,7 +113,7 @@
 
 
 def stack_kernel(
-    mine_ref, other_ref, src_ref, table_ref, edge_table_ref, member_ref, out_ref,
+    part0_ref, part1_ref, part2_ref, part3_ref, src_ref, table_ref, edge_table_ref, member_ref, out_ref,
     src_sc, cross_sc, prod_sc, edge_prod_sc, minus_sc, edge_sc, sums_sc,
 ):
     step_id = pl.program_id(0)
@@ -92,13 +135,13 @@
             for w in range(8):
                 half, wl = divmod(w, 4)
                 row = half * 8 + s * 4 + wl
-                ref = other_ref if half else mine_ref
+                ref = (part0_ref, part1_ref, part2_ref, part3_ref)[w // 2]
                 for g in range(3):
                     rows = slice(16 * g, 16 * g + 16)
                     sr = jnp.broadcast_to(src_sc[0, row : row + 1, :], (16, F))
                     si = jnp.broadcast_to(src_sc[1, row : row + 1, :], (16, F))
-                    wr = ref[0, wl, rows, :].astype(f32)
-                    wi = ref[1, wl, rows, :].astype(f32)
+                    wr = ref[0, w % 2, rows, :].astype(f32)
+                    wi = ref[1, w % 2, rows, :].astype(f32)
                     at = w * 48 + 16 * g
                     cross_sc[s, at : at + 16, :] = (wr * sr + wi * si).astype(bf16)
                     cross_sc[s, 384 + at : 384 + at + 16, :] = (wi * sr - wr * si).astype(bf16)
@@ -175,15 +218,14 @@
             out_ref[:, win, k] = binned.reshape(16, 8, HALF).astype(bf16)
 
 
-def stack_partial(mine, other, src, member):
+def stack_partial(parts, src, member):
     table, edge_table = lag_tables()
     whole = lambda *shape: pl.BlockSpec(shape, lambda b: (0,) * len(shape), pipeline_mode=pl.Buffered(1))
     return pl.pallas_call(
         stack_kernel,
         grid=(PAIRS,),
         in_specs=[
-            whole(2, 4, 48, F),
-            whole(2, 4, 48, F),
+            *[whole(2, 2, 48, F)] * 4,
             whole(32, F),
             pl.BlockSpec((1, F, 1024), lambda b: (PAIRS - 1 - b, 0, 0)),
             whole(F, 256),
@@ -202,7 +244,7 @@
         ],
         compiler_params=pltpu.CompilerParams(vmem_limit_bytes=48 << 20),
         name="stack",
-    )(mine, other, src, jnp.asarray(table), jnp.asarray(edge_table), member)
+    )(*parts, src, jnp.asarray(table), jnp.asarray(edge_table), member)
 
 
 def shift(count):
@@ -217,25 +259,21 @@
     swap = [(0, 1), (1, 0)]
     slot_rows = bin_rows[:, 0]
 
-    owners, rows = sources // chan_dev, sources % chan_dev
-    picked = [
-        jnp.where(owners[s] == chan, lax.dynamic_index_in_dim(spectra, rows[s], 0, keepdims=False), 0)
-        for s in range(4)
-    ]
-    counts = jnp.sum((slot_rows >= 0).astype(f32), axis=2).astype(bf16)
-    counts = jnp.pad(counts.reshape(1, 128), ((0, 7), (0, F - 128)))
-    sent = jnp.concatenate([jnp.stack(picked).reshape(32, F), counts], axis=0)
+    sent = pick(spectra, sources, jnp.transpose(bin_rows, (0, 3, 1, 2)))
+    flipped = jnp.transpose(spectra, (2, 1, 0, 3))
+    early, late = whiten(flipped[:, :2]), flipped[:, 2:]
     for axis in ("z", "y"):
         got = [lax.ppermute(sent, axis, shift(k)) for k in (1, 3, 2)]
         sent = (sent + got[0]) + (got[1] + got[2])
-    counts = sent[32, :128].astype(f32).reshape(4, NBINS)
-    src = sent[:32].reshape(2, 2, 4, 2, F)
+        if axis == "z":
+            sent, late = lax.optimization_barrier((sent, late))
+            late = whiten(late)
+    counts = sent[4, :, 0, :NBINS].astype(f32)
+    src = sent[:4].reshape(2, 2, 4, 2, F)
     src_mine = lax.dynamic_index_in_dim(src, c, 0, keepdims=False)
     src_other = lax.ppermute(lax.dynamic_index_in_dim(src, 1 - c, 0, keepdims=False), "c", swap)
     src = jnp.transpose(jnp.stack([src_mine, src_other]), (3, 0, 1, 2, 4)).reshape(32, F)
-
-    mine = whiten(jnp.transpose(spectra, (2, 1, 0, 3)))
-    other = lax.ppermute(mine, "c", swap)
+    parts = [early, late, lax.ppermute(early, "c", swap), lax.ppermute(late, "c", swap)]
 
     own_rows = lax.dynamic_slice_in_dim(slot_rows, 2 * c, 2, 0)
     member = jnp.any(own_rows[..., None] == jnp.arange(chan_dev), axis=2).reshape(2, 16, 2, chan_dev)
@@ -247,7 +285,7 @@
         * eye[None, None, :, None, None, :, None]
     ).reshape(128, 4 * chan_dev)
 
-    partial = stack_partial(mine, other, src, member)
+    partial = stack_partial(parts, src, member)
     received = lax.all_to_all(partial.reshape(64, 6, 8, HALF), ("y", "z", "x"), 0, 0, tiled=True)
     totals = jnp.sum(received.astype(f32), axis=0).reshape(2, 3, 2, 2, 2, HALF)
     counts = lax.dynamic_slice(counts, (2 * c, 2 * chan), (2, 2))

time: 98.2 us -> 85.2 us (0.87)
  between operations: 10.5 us -> 0.26 us
  waiting for transfers between devices: 28.6 us -> 25 us
  Pallas kernels: 27.9 us -> 31.4 us
  other arithmetic: 3.9 us -> 1.52 us
    ppermute x6, waiting for transfers between devices: 3.7 us -> 0.02 us  [shards(): got = [lax.ppermute(sent, axis, shift(k)) for k in (1, 3, 2)]]
    pallas_call x1 -> x2, Pallas kernels: 22.8 us -> 24.9 us  [the longest x1 22.8 us: stack_partial(): pl.pallas_call(stack_kernel, grid=(PAIRS,), in_specs=[*[whole(2, 2, 48, F...]
    select_n x2 -> x0, other arithmetic: 1.5 us -> none  [the longest x1 0.84 us: shards(): jnp.where(owners[s] == chan, lax.dynamic_index_in_dim(spectra, rows[s], 0...]
    pallas_call x1 -> x2, Pallas kernels: 5.09 us -> 6.44 us  [whiten(): pl.pallas_call(whiten_kernel, grid=(x.shape[1],), in_specs=[spec], out_sp...]
    ppermute x1 -> x2, starting transfers between devices: 1.52 us -> 2.39 us  [the longest x1 1.52 us: shards(): lax.ppermute(early, 'c', swap)]
    unnamed x8 -> x12, local copies, waits for them, and re-layouts: 2.48 us -> 1.6 us
  transfers between devices with their start and end apart: 10 -> 11, of which waited for: 6 -> 3; matrix products, arithmetic and copies ran while one was open for 4% -> 4% of each run, Pallas kernels for 5% -> 8%
where the time goes in v2:
time: 85.2 us; the launch traced here: 84.9 us
  Pallas kernels  31.4 us (37%)
  waiting for transfers between devices  25 us (29%)
  starting transfers between devices  23.5 us (28%)
  local copies, waits for them, and re-layouts  3.3 us (4%)
  other arithmetic  1.52 us (2%)
    all_to_all x1, waiting for transfers between devices, shards(): lax.all_to_all(partial.reshape(64, 6, 8, HALF), ('y', 'z', 'x'), 0, 0, ti...  23.6 us
    pallas_call x1, Pallas kernels, stack_partial(): pl.pallas_call(stack_kernel, grid=(PAIRS,), in_specs=[*[whole(2, 2, 48, F...  22.8 us
    ppermute x6, starting transfers between devices, shards(): got = [lax.ppermute(sent, axis, shift(k)) for k in (1, 3, 2)]  9.79 us
    all_to_all x1, starting transfers between devices, shards(): lax.all_to_all(partial.reshape(64, 6, 8, HALF), ('y', 'z', 'x'), 0, 0, ti...  7.89 us
    pallas_call x2, Pallas kernels, whiten(): pl.pallas_call(whiten_kernel, grid=(x.shape[1],), in_specs=[spec], out_sp...  6.44 us
    pallas_call x1, Pallas kernels, pick(): pl.pallas_call(pick_kernel, in_specs=[pl.BlockSpec(memory_space=pltpu.SME...  2.13 us
    ppermute x1, starting transfers between devices, shards(): got = lax.ppermute(send, 'c', swap)  1.98 us
  transfers between devices with their start and end apart: 11, of which 3 were waited for; matrix products, arithmetic and copies ran while one was open for 4% of the time, Pallas kernels for 8%

profile of v2, /device:TPU:1, one launch (start us, length us, event | category | flops | bytes accessed | tf_op | source)
XLA Modules:
  0.0 84.9 jit_solution(15953331987180970525)
XLA Ops:
  0.0 2.1 %pick.1 = bf16[5,4,2,1024]{3,2,1,0:T(2,128)(2,1)} custom-call(s32[4]{0:T(128)} %sources_ref.1, s32[4,3,1,32]{3,2,1,0:T(1,128)} %bitcast.78, bf16[48,4,2,1024]{3,2,1,0:T(2,128)(2,1)} %spectra_ref.1), custom_call_target="tpu_custom_call" | custom-call | tf_op jit(solution)/shard_map/pick/pallas_call | solution.py:79
  2.1 3.9 %collective-permute-start.2 = (bf16[5,4,2,1024]{3,2,1,0:T(2,128)(2,1)}, bf16[5,4,2,1024]{3,2,1,0:T(2,128)(2,1)S(1)}, u32[]{:S(2)}, u32[]{:S(2)}) collective-permute-start(bf16[5,4,2,1024]{3,2,1,0:T(2,128)(2,1)} %pick.1), channel_id=1, source_target_pairs={{0,16},{8,24},{16,0},{24,8},{1,17},{9,25},{17,1},{25,9},{2,18},{10... | collective-permute-start | bytes 245768 | tf_op jit(solution)/shard_map/ppermute | solution.py:266
  6.0 0.4 collective-permute-start.1
  6.4 1.0 %collective-permute-start = (bf16[5,4,2,1024]{3,2,1,0:T(2,128)(2,1)}, bf16[5,4,2,1024]{3,2,1,0:T(2,128)(2,1)S(1)}, u32[]{:S(2)}, u32[]{:S(2)}) collective-permute-start(bf16[5,4,2,1024]{3,2,1,0:T(2,128)(2,1)} %pick.1), channel_id=1, source_target_pairs={{0,8},{8,16},{16,24},{24,0},{1,9},{9,17},{17,25},{25,1},{2,10},{10... | collective-permute-start | bytes 245768 | tf_op jit(solution)/shard_map/ppermute | solution.py:266
  7.5 1.6 %copy.39 = bf16[48,4,2,1024]{3,0,1,2:T(8,128)(2,1)S(1)} copy(bf16[48,4,2,1024]{3,2,1,0:T(2,128)(2,1)} %spectra_ref.1) | data formatting | bytes 1572864 | tf_op args[0]
  9.0 0.0 copy-start.4
  9.1 0.0 copy-start.3
  9.1 1.0 %fusion.10 = (bf16[2,2,48,1024]{3,2,1,0:T(8,128)(2,1)}, bf16[2,2,48,1024]{3,2,1,0:T(8,128)(2,1)}) fusion(bf16[2,4,48,1024]{3,2,1,0:T(8,128)(2,1)S(1)} %bitcast.59), kind=kLoop, calls=%fused_computation.33 | loop fusion | bytes 1572864 | tf_op jit(solution)/shard_map/slice | solution.py:264
  10.0 3.2 %whiten.2.part0_ref = bf16[2,2,48,1024]{3,2,1,0:T(8,128)(2,1)} custom-call(bf16[2,2,48,1024]{3,2,1,0:T(8,128)(2,1)} %get-tuple-element.10.x_ref), custom_call_target="tpu_custom_call" | custom-call | tf_op jit(solution)/shard_map/whiten/pallas_call | solution.py:105
  13.2 0.0 copy-start
  13.2 0.0 copy-start.2
  13.2 1.5 %collective-permute-start.3 = (bf16[2,2,48,1024]{3,2,1,0:T(8,128)(2,1)}, bf16[2,2,48,1024]{3,2,1,0:T(8,128)(2,1)S(1)}, u32[]{:S(2)}, u32[]{:S(2)}) collective-permute-start(bf16[2,2,48,1024]{3,2,1,0:T(8,128)(2,1)} %whiten.2.part0_ref), channel_id=1, source_target_pairs={{0,1},{1,0},{2,3},{3,2},{4,5},{5,4},{6,7},{7,6},{8,9},{9,8},{10,11... | collective-permute-start | bytes 1179656 | tf_op jit(solution)/shard_map/ppermute | solution.py:276
  14.7 0.0 copy-done.4
  14.8 0.1 fusion
  14.9 0.0 collective-permute-done.2
  14.9 0.0 collective-permute-done.1
  14.9 0.0 collective-permute-done
  14.9 0.0 copy-done.3
  15.0 3.0 %collective-permute-start.7 = (bf16[5,4,2,1024]{3,2,1,0:T(2,128)(2,1)S(1)}, bf16[5,4,2,1024]{3,2,1,0:T(2,128)(2,1)S(1)}, u32[]{:S(2)}, u32[]{:S(2)}) collective-permute-start(bf16[5,4,2,1024]{3,2,1,0:T(2,128)(2,1)S(1)} %bitcast.61), channel_id=1, source_target_pairs={{0,64},{32,96},{64,0},{96,32},{1,65},{33,97},{65,1},{97,33},{2,66}... | collective-permute-start | bytes 245768 | tf_op jit(solution)/shard_map/ppermute | solution.py:266
  18.0 0.8 collective-permute-start.6
  18.7 0.7 collective-permute-start.5
  19.4 0.1 broadcast_multiply_fusion.1
  19.5 3.2 %whiten.3.part1_ref = bf16[2,2,48,1024]{3,2,1,0:T(8,128)(2,1)} custom-call(bf16[2,2,48,1024]{3,2,1,0:T(8,128)(2,1)} %get-tuple-element.7.x_ref), custom_call_target="tpu_custom_call" | custom-call | tf_op jit(solution)/shard_map/whiten/pallas_call | solution.py:105
  22.8 0.0 copy-start.1
  22.8 0.9 %collective-permute-start.4 = (bf16[2,2,48,1024]{3,2,1,0:T(8,128)(2,1)}, bf16[2,2,48,1024]{3,2,1,0:T(8,128)(2,1)S(1)}, u32[]{:S(2)}, u32[]{:S(2)}) collective-permute-start(bf16[2,2,48,1024]{3,2,1,0:T(8,128)(2,1)} %whiten.3.part1_ref), channel_id=1, source_target_pairs={{0,1},{1,0},{2,3},{3,2},{4,5},{5,4},{6,7},{7,6},{8,9},{9,8},{10,11... | collective-permute-start | bytes 1179656 | tf_op jit(solution)/shard_map/ppermute | solution.py:276
  23.6 0.0 collective-permute-done.7
  23.7 0.0 collective-permute-done.6
  23.7 0.0 collective-permute-done.5
  23.7 0.1 constant_dynamic-slice_fusion.4
  23.8 1.4 %collective-permute-start.8 = (bf16[2,4,2,1024]{3,1,0,2:T(4,128)(2,1)S(1)}, bf16[2,4,2,1024]{3,1,0,2:T(4,128)(2,1)S(1)}, u32[]{:S(2)}, u32[]{:S(2)}) collective-permute-start(bf16[2,4,2,1024]{3,1,0,2:T(4,128)(2,1)S(1)} %bitcast.76), channel_id=1, source_target_pairs={{0,1},{1,0},{2,3},{3,2},{4,5},{5,4},{6,7},{7,6},{8,9},{9,8},{10,11... | collective-permute-start | bytes 98312 | tf_op jit(solution)/shard_map/ppermute | solution.py:274
  25.2 0.2 broadcast_multiply_fusion
  25.4 0.1 mul.78.member_ref
  25.6 0.5 collective-permute-done.8
  26.2 0.0 collective-permute-done.3.part2_ref
  26.2 0.0 collective-permute-done.4.part3_ref
  26.2 0.0 copy-done
  26.2 0.0 copy-done.2
  26.2 0.0 copy-done.1
  26.2 22.8 %stack.25 = bf16[16,8,3,8,256]{4,3,2,1,0:T(8,128)(2,1)} custom-call(bf16[2,2,48,1024]{3,2,1,0:T(8,128)(2,1)S(1)} %copy-done, bf16[2,2,48,1024]{3,2,1,0:T(8,128)(2,1)S(1)} %copy-done.1, bf16[2,2,48,1024]{3,2,1,0:T(8,128)(2,1)S(1)} %collective-permute-done.3.part2_ref, bf16[2,2,48,1024]{3,2,1,0:T(8,128)(2,1)S(1)} %collective-permute-done.4.part3_ref, ...), custom_call_target="tpu_custom_call" | custom-call | tf_op jit(solution)/shard_map/stack/pallas_call | solution.py:224
  49.0 7.9 %all-to-all-start = ((bf16[64,6,8,256]{3,2,1,0:T(8,128)(2,1)}), bf16[64,6,8,256]{3,2,1,0:T(8,128)(2,1)S(1)}, u32[]{:S(2)}, u32[]{:S(2)}) async-start(bf16[64,6,8,256]{3,2,1,0:T(8,128)(2,1)} %bitcast.9), calls=%async_computation | async-start | bytes 3145728 | tf_op jit(solution)/shard_map/all_to_all | solution.py:289
  56.9 0.1 fusion.9
  57.0 23.6 %all-to-all-done = bf16[64,6,8,256]{3,2,1,0:T(8,128)(2,1)S(1)} async-done(((bf16[64,6,8,256]{3,2,1,0:T(8,128)(2,1)}), bf16[64,6,8,256]{3,2,1,0:T(8,128)(2,1)S(1)}, u32[]{:S(2)}, u32[]{:S(2)}) %all-to-all-start) | async-done | bytes 1572896 | tf_op jit(solution)/shard_map/all_to_all | solution.py:289
  80.6 0.2 convert_reduce_fusion
  80.9 0.1 fusion.6
  81.0 2.0 %collective-permute-start.9 = (f32[2,2,2,256]{3,2,1,0:T(2,128)S(1)}, f32[2,2,2,256]{3,2,1,0:T(2,128)S(1)}, u32[]{:S(2)}, u32[]{:S(2)}) collective-permute-start(f32[2,2,2,256]{3,2,1,0:T(2,128)S(1)} %get-tuple-element.14), channel_id=1, source_target_pairs={{0,1},{1,0},{2,3},{3,2},{4,5},{5,4},{6,7},{7,6},{8,9},{9,8},{10,11... | collective-permute-start | bytes 24584 | tf_op jit(solution)/shard_map/ppermute | solution.py:297
  83.0 0.8 collective-permute-done.9
  83.9 0.4 rev.3
  84.3 0.6 broadcast_select_fusion
  (19 shorter events, 0.3 us)
Async XLA Ops:
  2.1 12.8 %collective-permute-start.2 = (bf16[5,4,2,1024]{3,2,1,0:T(2,128)(2,1)}, bf16[5,4,2,1024]{3,2,1,0:T(2,128)(2,1)S(1)}, u32[]{:S(2)}, u32[]{:S(2)}) collective-permute-start(bf16[5,4,2,1024]{3,2,1,0:T(2,128)(2,1)} %pick.1), channel_id=1, source_target_pairs={{0,16},{8,24},{16,0},{24,8},{1,17},{9,25},{17,1},{25,9},{2,18},{10... | collective-permute-start | bytes 245768 | tf_op jit(solution)/shard_map/ppermute | solution.py:266
  6.0 8.9 %collective-permute-start.1 = (bf16[5,4,2,1024]{3,2,1,0:T(2,128)(2,1)}, bf16[5,4,2,1024]{3,2,1,0:T(2,128)(2,1)S(1)}, u32[]{:S(2)}, u32[]{:S(2)}) collective-permute-start(bf16[5,4,2,1024]{3,2,1,0:T(2,128)(2,1)} %pick.1), channel_id=1, source_target_pairs={{0,24},{8,0},{16,8},{24,16},{1,25},{9,1},{17,9},{25,17},{2,26},{10... | collective-permute-start | bytes 245768 | tf_op jit(solution)/shard_map/ppermute | solution.py:266
  6.4 8.5 %collective-permute-start = (bf16[5,4,2,1024]{3,2,1,0:T(2,128)(2,1)}, bf16[5,4,2,1024]{3,2,1,0:T(2,128)(2,1)S(1)}, u32[]{:S(2)}, u32[]{:S(2)}) collective-permute-start(bf16[5,4,2,1024]{3,2,1,0:T(2,128)(2,1)} %pick.1), channel_id=1, source_target_pairs={{0,8},{8,16},{16,24},{24,0},{1,9},{9,17},{17,25},{25,1},{2,10},{10... | collective-permute-start | bytes 245768 | tf_op jit(solution)/shard_map/ppermute | solution.py:266
  9.0 5.7 %copy-start.4 = (s32[4,1,32,3]{2,1,3,0:T(1,128)S(1)}, s32[4,1,32,3]{2,1,3,0:T(1,128)}, u32[]{:S(2)}) copy-start(s32[4,1,32,3]{2,1,3,0:T(1,128)} %param.7) | copy-start | bytes 4612
  9.1 5.9 %copy-start.3 = (bf16[5,4,2,1024]{3,2,1,0:T(2,128)(2,1)S(1)}, bf16[5,4,2,1024]{3,2,1,0:T(2,128)(2,1)}, u32[]{:S(2)}) copy-start(bf16[5,4,2,1024]{3,2,1,0:T(2,128)(2,1)} %pick.1) | copy-start | bytes 245764
  13.2 13.0 %copy-start = (bf16[2,2,48,1024]{3,2,1,0:T(8,128)(2,1)S(1)}, bf16[2,2,48,1024]{3,2,1,0:T(8,128)(2,1)}, u32[]{:S(2)}) copy-start(bf16[2,2,48,1024]{3,2,1,0:T(8,128)(2,1)} %whiten.2.part0_ref) | copy-start | bytes 1179652
  13.2 13.0 %copy-start.2 = (bf16[1024,256]{1,0:T(8,128)(2,1)S(1)}, bf16[1024,256]{1,0:T(8,128)(2,1)}, u32[]{:S(2)}) copy-start(bf16[1024,256]{1,0:T(8,128)(2,1)} %constant.56.clone.edge_table_ref) | copy-start | bytes 1572868
  13.2 12.9 %collective-permute-start.3 = (bf16[2,2,48,1024]{3,2,1,0:T(8,128)(2,1)}, bf16[2,2,48,1024]{3,2,1,0:T(8,128)(2,1)S(1)}, u32[]{:S(2)}, u32[]{:S(2)}) collective-permute-start(bf16[2,2,48,1024]{3,2,1,0:T(8,128)(2,1)} %whiten.2.part0_ref), channel_id=1, source_target_pairs={{0,1},{1,0},{2,3},{3,2},{4,5},{5,4},{6,7},{7,6},{8,9},{9,8},{10,11... | collective-permute-start | bytes 1179656 | tf_op jit(solution)/shard_map/ppermute | solution.py:276
  15.0 8.7 %collective-permute-start.7 = (bf16[5,4,2,1024]{3,2,1,0:T(2,128)(2,1)S(1)}, bf16[5,4,2,1024]{3,2,1,0:T(2,128)(2,1)S(1)}, u32[]{:S(2)}, u32[]{:S(2)}) collective-permute-start(bf16[5,4,2,1024]{3,2,1,0:T(2,128)(2,1)S(1)} %bitcast.61), channel_id=1, source_target_pairs={{0,64},{32,96},{64,0},{96,32},{1,65},{33,97},{65,1},{97,33},{2,66}... | collective-permute-start | bytes 245768 | tf_op jit(solution)/shard_map/ppermute | solution.py:266
  18.0 5.7 %collective-permute-start.6 = (bf16[5,4,2,1024]{3,2,1,0:T(2,128)(2,1)S(1)}, bf16[5,4,2,1024]{3,2,1,0:T(2,128)(2,1)S(1)}, u32[]{:S(2)}, u32[]{:S(2)}) collective-permute-start(bf16[5,4,2,1024]{3,2,1,0:T(2,128)(2,1)S(1)} %bitcast.62), channel_id=1, source_target_pairs={{0,96},{32,0},{64,32},{96,64},{1,97},{33,1},{65,33},{97,65},{2,98}... | collective-permute-start | bytes 245768 | tf_op jit(solution)/shard_map/ppermute | solution.py:266
  18.7 4.9 %collective-permute-start.5 = (bf16[5,4,2,1024]{3,2,1,0:T(2,128)(2,1)S(1)}, bf16[5,4,2,1024]{3,2,1,0:T(2,128)(2,1)S(1)}, u32[]{:S(2)}, u32[]{:S(2)}) collective-permute-start(bf16[5,4,2,1024]{3,2,1,0:T(2,128)(2,1)S(1)} %bitcast.63), channel_id=1, source_target_pairs={{0,32},{32,64},{64,96},{96,0},{1,33},{33,65},{65,97},{97,1},{2,34}... | collective-permute-start | bytes 245768 | tf_op jit(solution)/shard_map/ppermute | solution.py:266
  22.8 3.4 %copy-start.1 = (bf16[2,2,48,1024]{3,2,1,0:T(8,128)(2,1)S(1)}, bf16[2,2,48,1024]{3,2,1,0:T(8,128)(2,1)}, u32[]{:S(2)}) copy-start(bf16[2,2,48,1024]{3,2,1,0:T(8,128)(2,1)} %whiten.3.part1_ref) | copy-start | bytes 1179652
  22.8 3.4 %collective-permute-start.4 = (bf16[2,2,48,1024]{3,2,1,0:T(8,128)(2,1)}, bf16[2,2,48,1024]{3,2,1,0:T(8,128)(2,1)S(1)}, u32[]{:S(2)}, u32[]{:S(2)}) collective-permute-start(bf16[2,2,48,1024]{3,2,1,0:T(8,128)(2,1)} %whiten.3.part1_ref), channel_id=1, source_target_pairs={{0,1},{1,0},{2,3},{3,2},{4,5},{5,4},{6,7},{7,6},{8,9},{9,8},{10,11... | collective-permute-start | bytes 1179656 | tf_op jit(solution)/shard_map/ppermute | solution.py:276
  23.8 2.3 %collective-permute-start.8 = (bf16[2,4,2,1024]{3,1,0,2:T(4,128)(2,1)S(1)}, bf16[2,4,2,1024]{3,1,0,2:T(4,128)(2,1)S(1)}, u32[]{:S(2)}, u32[]{:S(2)}) collective-permute-start(bf16[2,4,2,1024]{3,1,0,2:T(4,128)(2,1)S(1)} %bitcast.76), channel_id=1, source_target_pairs={{0,1},{1,0},{2,3},{3,2},{4,5},{5,4},{6,7},{7,6},{8,9},{9,8},{10,11... | collective-permute-start | bytes 98312 | tf_op jit(solution)/shard_map/ppermute | solution.py:274
  49.0 31.6 %all-to-all-start = ((bf16[64,6,8,256]{3,2,1,0:T(8,128)(2,1)}), bf16[64,6,8,256]{3,2,1,0:T(8,128)(2,1)S(1)}, u32[]{:S(2)}, u32[]{:S(2)}) async-start(bf16[64,6,8,256]{3,2,1,0:T(8,128)(2,1)} %bitcast.9), calls=%async_computation | async-start | bytes 3145728 | tf_op jit(solution)/shard_map/all_to_all | solution.py:289
  81.0 2.8 %collective-permute-start.9 = (f32[2,2,2,256]{3,2,1,0:T(2,128)S(1)}, f32[2,2,2,256]{3,2,1,0:T(2,128)S(1)}, u32[]{:S(2)}, u32[]{:S(2)}) collective-permute-start(f32[2,2,2,256]{3,2,1,0:T(2,128)S(1)} %get-tuple-element.14), channel_id=1, source_target_pairs={{0,1},{1,0},{2,3},{3,2},{4,5},{5,4},{6,7},{7,6},{8,9},{9,8},{10,11... | collective-permute-start | bytes 24584 | tf_op jit(solution)/shard_map/ppermute | solution.py:297

commit v3 on v2

--- a/solution.py
+++ b/solution.py
@@ -51,7 +51,7 @@
     me = lax.axis_index("y") * 4 + lax.axis_index("z")
     for s in range(4):
         owner, row = sources_ref[s] // 48, sources_ref[s] % 48
-        copy = pltpu.make_async_copy(spectra_ref.at[row], out_ref.at[s], sem.at[s])
+        copy = pltpu.make_async_copy(spectra_ref.at[row], out_ref.at[s, :, :, pl.ds(0, F)], sem.at[s])
 
         @pl.when(owner == me)
         def _(copy=copy):
@@ -59,16 +59,16 @@
 
         @pl.when(owner != me)
         def _(s=s):
-            out_ref[s] = jnp.zeros((4, 2, F), bf16)
-
-    out_ref[4] = jnp.zeros((4, 2, F), bf16)
-    for s in range(4):
+            out_ref[s, :, :, :F] = jnp.zeros((4, 2, F), bf16)
+
         live = (slots_ref[s] >= 0).astype(f32)
         count = live[0] + live[1] + live[2]
-        out_ref[4, s, :, :NBINS] = jnp.broadcast_to(count, (2, NBINS)).astype(bf16)
+        out_ref[s, :, :, F:] = jnp.zeros((4, 2, 128), bf16)
+        out_ref[s, 0, :, F : F + NBINS] = jnp.broadcast_to(count, (2, NBINS)).astype(bf16)
+
     for s in range(4):
         owner, row = sources_ref[s] // 48, sources_ref[s] % 48
-        copy = pltpu.make_async_copy(spectra_ref.at[row], out_ref.at[s], sem.at[s])
+        copy = pltpu.make_async_copy(spectra_ref.at[row], out_ref.at[s, :, :, pl.ds(0, F)], sem.at[s])
 
         @pl.when(owner == me)
         def _(copy=copy):
@@ -84,41 +84,73 @@
             pl.BlockSpec(memory_space=pl.ANY),
         ],
         out_specs=pl.BlockSpec(memory_space=pltpu.VMEM),
-        out_shape=jax.ShapeDtypeStruct((5, 4, 2, F), bf16),
+        out_shape=jax.ShapeDtypeStruct((4, 4, 2, F + 128), bf16),
         scratch_shapes=[pltpu.SemaphoreType.DMA((4,))],
         name="pick",
     )(sources, slots, spectra)
 
 
-def whiten_kernel(x_ref, o_ref):
-    for g in range(3):
-        rows = slice(16 * g, 16 * g + 16)
-        re = x_ref[0, 0, rows, :].astype(f32)
-        im = x_ref[1, 0, rows, :].astype(f32)
-        inv = 1.0 / smooth_amplitude(re, im)
-        o_ref[0, 0, rows, :] = (re * inv).astype(bf16)
-        o_ref[1, 0, rows, :] = (im * inv).astype(bf16)
-
-
-def whiten(x):
-    spec = pl.BlockSpec((2, 1, 48, F), lambda w: (0, w, 0, 0))
+def whiten_kernel(x_ref, band_ref, o_ref, amp_sc):
+    edge = jnp.zeros((384, 128), bf16)
+    amp_sc[:, :128] = edge
+    amp_sc[:, 128 + F :] = edge
+    for w in range(4):
+        re = x_ref[0, w].astype(f32)
+        im = x_ref[1, w].astype(f32)
+        amp = jnp.sqrt(re * re + im * im)
+        high = amp.astype(bf16)
+        amp_sc[48 * w : 48 * w + 48, 128 : 128 + F] = high
+        amp_sc[192 + 48 * w : 192 + 48 * w + 48, 128 : 128 + F] = (amp - high.astype(f32)).astype(bf16)
+    for n in range(4):
+        lanes = slice(256 * n, 256 * n + 256)
+        total = jnp.dot(amp_sc[:, 256 * n : 256 * n + 512], band_ref[...], preferred_element_type=f32)
+        total = (total[:192] + total[192:]) * (1.0 / (2 * HW + 1)) + EPS
+        inv = 1.0 / total
+        for w in range(4):
+            part = inv[48 * w : 48 * w + 48]
+            o_ref[0, w, :, lanes] = (x_ref[0, w, :, lanes].astype(f32) * part).astype(bf16)
+            o_ref[1, w, :, lanes] = (x_ref[1, w, :, lanes].astype(f32) * part).astype(bf16)
+
+
+def whiten(x, band):
+    vmem = pl.BlockSpec(memory_space=pltpu.VMEM)
     return pl.pallas_call(
         whiten_kernel,
-        grid=(x.shape[1],),
-        in_specs=[spec],
-        out_specs=spec,
+        in_specs=[vmem, vmem],
+        out_specs=vmem,
         out_shape=jax.ShapeDtypeStruct(x.shape, bf16),
+        scratch_shapes=[pltpu.VMEM((384, F + 256), bf16)],
+        cost_estimate=pl.CostEstimate(flops=8 * 10**8, bytes_accessed=2 * 10**6, transcendentals=4 * 10**5),
         name="whiten",
-    )(x)
+    )(x, band)
 
 
 def stack_kernel(
-    part0_ref, part1_ref, part2_ref, part3_ref, src_ref, table_ref, edge_table_ref, member_ref, out_ref,
-    src_sc, cross_sc, prod_sc, edge_prod_sc, minus_sc, edge_sc, sums_sc,
+    mine_ref, other_ref, src_ref, table_ref, edge_table_ref, member_ref, out_ref,
+    src_sc, cross_sc, prod_sc, edge_prod_sc, minus_sc, edge_sc, sums_sc, table_sc, table_sem, part_sc, part_sem,
 ):
     step_id = pl.program_id(0)
     block = PAIRS - 1 - step_id
     floor2 = (FLOOR * 32.0) ** 2
+    slot = step_id % 2
+
+    def fetch(step):
+        return pltpu.make_async_copy(table_ref.at[PAIRS - 1 - step], table_sc.at[step % 2], table_sem.at[step % 2])
+
+    parts = [
+        pltpu.make_async_copy(ref, part_sc.at[i], part_sem.at[i])
+        for i, ref in enumerate((mine_ref, other_ref))
+    ]
+
+    @pl.when(step_id == 0)
+    def _():
+        for copy in parts:
+            copy.start()
+        fetch(0).start()
+
+    @pl.when(step_id < PAIRS - 1)
+    def _():
+        fetch(step_id + 1).start()
 
     def unit(re, im):
         inv = lax.rsqrt(jnp.maximum(re * re + im * im, floor2))
@@ -131,17 +163,19 @@
         inv = 1.0 / smooth_amplitude(re, im)
         src_sc[0] = (re * inv).astype(bf16).astype(f32)
         src_sc[1] = (im * inv).astype(bf16).astype(f32)
-        for s in range(2):
-            for w in range(8):
-                half, wl = divmod(w, 4)
+        for w in range(8):
+            half, wl = divmod(w, 4)
+            if wl == 0:
+                parts[half].wait()
+            for s in range(2):
                 row = half * 8 + s * 4 + wl
-                ref = (part0_ref, part1_ref, part2_ref, part3_ref)[w // 2]
+                ref = part_sc.at[half]
                 for g in range(3):
                     rows = slice(16 * g, 16 * g + 16)
                     sr = jnp.broadcast_to(src_sc[0, row : row + 1, :], (16, F))
                     si = jnp.broadcast_to(src_sc[1, row : row + 1, :], (16, F))
-                    wr = ref[0, w % 2, rows, :].astype(f32)
-                    wi = ref[1, w % 2, rows, :].astype(f32)
+                    wr = ref[0, wl, rows, :].astype(f32)
+                    wi = ref[1, wl, rows, :].astype(f32)
                     at = w * 48 + 16 * g
                     cross_sc[s, at : at + 16, :] = (wr * sr + wi * si).astype(bf16)
                     cross_sc[s, 384 + at : 384 + at + 16, :] = (wi * sr - wr * si).astype(bf16)
@@ -165,7 +199,7 @@
     def product(i):
         h, s = divmod(i, 2)
         prod_sc[i % 2] = jnp.dot(
-            cross_sc[s], table_ref[0, :, h * 512 : h * 512 + 512], preferred_element_type=f32
+            cross_sc[s], table_sc[slot, :, h * 512 : h * 512 + 512], preferred_element_type=f32
         )
 
     def epilogue(i):
@@ -195,6 +229,7 @@
                     lo = 256 * h + 128 * t
                     minus_sc[k, s, 16 * g : 16 * g + 16, lo : lo + 128] = value
 
+    fetch(step_id).wait()
     product(0)
     for i in range(1, 4):
         product(i)
@@ -220,18 +255,13 @@
 
 def stack_partial(parts, src, member):
     table, edge_table = lag_tables()
-    whole = lambda *shape: pl.BlockSpec(shape, lambda b: (0,) * len(shape), pipeline_mode=pl.Buffered(1))
+    hbm = pl.BlockSpec(memory_space=pl.ANY)
+    vmem = pl.BlockSpec(memory_space=pltpu.VMEM)
     return pl.pallas_call(
         stack_kernel,
         grid=(PAIRS,),
-        in_specs=[
-            *[whole(2, 2, 48, F)] * 4,
-            whole(32, F),
-            pl.BlockSpec((1, F, 1024), lambda b: (PAIRS - 1 - b, 0, 0)),
-            whole(F, 256),
-            whole(128, 192),
-        ],
-        out_specs=whole(16, 8, 3, 8, HALF),
+        in_specs=[hbm, hbm, vmem, hbm, vmem, vmem],
+        out_specs=vmem,
         out_shape=jax.ShapeDtypeStruct((16, 8, 3, 8, HALF), bf16),
         scratch_shapes=[
             pltpu.VMEM((2, 16, F), f32),
@@ -241,14 +271,24 @@
             pltpu.VMEM((3, 2, 48, BLOCK), f32),
             pltpu.VMEM((3, 2, 48, 128), f32),
             pltpu.VMEM((2, 3, 192, HALF), bf16),
+            pltpu.VMEM((2, F, 1024), bf16),
+            pltpu.SemaphoreType.DMA((2,)),
+            pltpu.VMEM((2, 2, 4, 48, F), bf16),
+            pltpu.SemaphoreType.DMA((2,)),
         ],
         compiler_params=pltpu.CompilerParams(vmem_limit_bytes=48 << 20),
+        cost_estimate=pl.CostEstimate(flops=14 * 10**9, bytes_accessed=12 * 10**6, transcendentals=6 * 10**6),
         name="stack",
     )(*parts, src, jnp.asarray(table), jnp.asarray(edge_table), member)
 
 
-def shift(count):
-    return [(i, (i + count) % 4) for i in range(4)]
+def crossed(count, stage):
+    pairs = []
+    for y, z, x, c in np.ndindex(4, 4, 4, 2):
+        along_z = c == stage
+        to = (y, (z + count) % 4) if along_z else ((y + count) % 4, z)
+        pairs.append((((y * 4 + z) * 4 + x) * 2 + c, ((to[0] * 4 + to[1]) * 4 + x) * 2 + c))
+    return pairs
 
 
 def shards(spectra, sources, bin_rows):
@@ -261,19 +301,19 @@
 
     sent = pick(spectra, sources, jnp.transpose(bin_rows, (0, 3, 1, 2)))
     flipped = jnp.transpose(spectra, (2, 1, 0, 3))
-    early, late = whiten(flipped[:, :2]), flipped[:, 2:]
-    for axis in ("z", "y"):
-        got = [lax.ppermute(sent, axis, shift(k)) for k in (1, 3, 2)]
+    band = np.abs(np.arange(512)[:, None] - 128 - np.arange(256)[None, :]) <= HW
+    for stage in range(2):
+        got = [lax.ppermute(sent, ("y", "z", "x", "c"), crossed(k, stage)) for k in (1, 3, 2)]
         sent = (sent + got[0]) + (got[1] + got[2])
-        if axis == "z":
-            sent, late = lax.optimization_barrier((sent, late))
-            late = whiten(late)
-    counts = sent[4, :, 0, :NBINS].astype(f32)
-    src = sent[:4].reshape(2, 2, 4, 2, F)
+        if stage == 0:
+            sent, flipped = lax.optimization_barrier((sent, flipped))
+            mine = whiten(flipped, jnp.asarray(band.astype(bf16)))
+    counts = sent[:, 0, 0, F : F + NBINS].astype(f32)
+    src = sent[..., :F].reshape(2, 2, 4, 2, F)
     src_mine = lax.dynamic_index_in_dim(src, c, 0, keepdims=False)
     src_other = lax.ppermute(lax.dynamic_index_in_dim(src, 1 - c, 0, keepdims=False), "c", swap)
     src = jnp.transpose(jnp.stack([src_mine, src_other]), (3, 0, 1, 2, 4)).reshape(32, F)
-    parts = [early, late, lax.ppermute(early, "c", swap), lax.ppermute(late, "c", swap)]
+    parts = [mine, lax.ppermute(mine, "c", swap)]
 
     own_rows = lax.dynamic_slice_in_dim(slot_rows, 2 * c, 2, 0)
     member = jnp.any(own_rows[..., None] == jnp.arange(chan_dev), axis=2).reshape(2, 16, 2, chan_dev)

time: 85.2 us -> 82.8 us (0.972)
  Pallas kernels: 31.4 us -> 26.7 us
  local copies, waits for them, and re-layouts: 3.3 us -> 5.03 us
    pallas_call x3 -> x2, Pallas kernels: 29.2 us -> 24.6 us  [the longest x1 21.7 us: stack_partial(): pl.pallas_call(stack_kernel, grid=(PAIRS,), in_specs=[hbm, hbm, vmem, hbm...]
    unnamed x12 -> x8, local copies, waits for them, and re-layouts: 1.6 us -> 3.6 us
    slice x3 -> x2, local copies, waits for them, and re-layouts: 1.01 us -> 0.05 us  [the longest x1 0.05 us: shards(): src = sent[..., :F].reshape(2, 2, 4, 2, F)]
    ppermute x8 -> x7, starting transfers between devices: 12.2 us -> 12.9 us  [the longest x6 9.83 us: shards(): lax.ppermute(sent, ('y', 'z', 'x', 'c'), crossed(k, stage))]
  transfers between devices with their start and end apart: 11 -> 10, of which waited for: 3 -> 4; matrix products, arithmetic and copies ran while one was open for 4% -> 5% of each run, Pallas kernels for 8% -> 4%
where the time goes in v3:
time: 82.8 us; the launch traced here: 82.7 us
  Pallas kernels  26.7 us (32%)
  waiting for transfers between devices  25.4 us (31%)
  starting transfers between devices  23.7 us (29%)
  local copies, waits for them, and re-layouts  5.03 us (6%)
  other arithmetic  1.53 us (2%)
    all_to_all x1, waiting for transfers between devices, shards(): lax.all_to_all(partial.reshape(64, 6, 8, HALF), ('y', 'z', 'x'), 0, 0, ti...  23.5 us
    pallas_call x1, Pallas kernels, stack_partial(): pl.pallas_call(stack_kernel, grid=(PAIRS,), in_specs=[hbm, hbm, vmem, hbm...  21.7 us
    ppermute x6, starting transfers between devices, shards(): lax.ppermute(sent, ('y', 'z', 'x', 'c'), crossed(k, stage))  9.83 us
    all_to_all x1, starting transfers between devices, shards(): lax.all_to_all(partial.reshape(64, 6, 8, HALF), ('y', 'z', 'x'), 0, 0, ti...  7.06 us
    unnamed x8, local copies, waits for them, and re-layouts  3.6 us
    ppermute x1, starting transfers between devices, shards(): parts = [mine, lax.ppermute(mine, 'c', swap)]  3.05 us
    pallas_call x1, Pallas kernels, whiten(): pl.pallas_call(whiten_kernel, in_specs=[vmem, vmem], out_specs=vmem, out_...  2.91 us
    pallas_call x1, Pallas kernels, pick(): pl.pallas_call(pick_kernel, in_specs=[pl.BlockSpec(memory_space=pltpu.SME...  2.12 us
  transfers between devices with their start and end apart: 10, of which 4 were waited for; matrix products, arithmetic and copies ran while one was open for 5% of the time, Pallas kernels for 4%

profile of v3, /device:TPU:1, one launch (start us, length us, event | category | flops | bytes accessed | tf_op | source)
XLA Modules:
  0.0 82.7 jit_solution(5396540216306342425)
XLA Ops:
  0.0 2.1 %pick.1 = bf16[4,4,2,1152]{3,2,1,0:T(2,128)(2,1)} custom-call(s32[4]{0:T(128)} %sources_ref.1, s32[4,3,1,32]{3,2,1,0:T(1,128)} %bitcast.78, bf16[48,4,2,1024]{3,2,1,0:T(2,128)(2,1)} %spectra_ref.1), custom_call_target="tpu_custom_call" | custom-call | tf_op jit(solution)/shard_map/pick/pallas_call | solution.py:79
  2.1 0.0 copy-start.2
  2.1 3.2 %collective-permute-start.2 = (bf16[4,4,2,1152]{3,2,1,0:T(2,128)(2,1)}, bf16[4,4,2,1152]{3,2,1,0:T(2,128)(2,1)S(1)}, u32[]{:S(2)}, u32[]{:S(2)}) collective-permute-start(bf16[4,4,2,1152]{3,2,1,0:T(2,128)(2,1)} %pick.1), channel_id=1, source_target_pairs={{0,16},{1,65},{2,18},{3,67},{4,20},{5,69},{6,22},{7,71},{8,24},{9,... | collective-permute-start | bytes 221192 | tf_op jit(solution)/shard_map/ppermute | solution.py:306
  5.4 0.8 collective-permute-start.1
  6.1 0.7 collective-permute-start
  6.8 0.7 constant_dynamic-slice_fusion.2
  7.5 0.1 fusion
  7.6 0.1 broadcast_multiply_fusion.1
  7.8 2.4 %copy.40 = bf16[48,4,2,1024]{3,0,1,2:T(8,128)(2,1)} copy(bf16[48,4,2,1024]{3,2,1,0:T(2,128)(2,1)} %spectra_ref.1) | data formatting | bytes 1572864 | tf_op args[0]
  10.2 0.0 collective-permute-done.2
  10.2 0.0 collective-permute-done.1
  10.2 0.5 collective-permute-done
  10.8 0.0 copy-done.2
  10.8 0.0 copy-start.1
  10.8 3.7 %collective-permute-start.6 = (bf16[4,4,2,1152]{3,2,1,0:T(2,128)(2,1)S(1)}, bf16[4,4,2,1152]{3,2,1,0:T(2,128)(2,1)S(1)}, u32[]{:S(2)}, u32[]{:S(2)}) collective-permute-start(bf16[4,4,2,1152]{3,2,1,0:T(2,128)(2,1)S(1)} %bitcast.61), channel_id=1, source_target_pairs={{0,64},{1,17},{2,66},{3,19},{4,68},{5,21},{6,70},{7,23},{8,72},{9,... | collective-permute-start | bytes 221192 | tf_op jit(solution)/shard_map/ppermute | solution.py:306
  14.5 0.9 %collective-permute-start.5 = (bf16[4,4,2,1152]{3,2,1,0:T(2,128)(2,1)S(1)}, bf16[4,4,2,1152]{3,2,1,0:T(2,128)(2,1)S(1)}, u32[]{:S(2)}, u32[]{:S(2)}) collective-permute-start(bf16[4,4,2,1152]{3,2,1,0:T(2,128)(2,1)S(1)} %bitcast.62), channel_id=1, source_target_pairs={{0,96},{1,25},{2,98},{3,27},{4,100},{5,29},{6,102},{7,31},{8,104},... | collective-permute-start | bytes 221192 | tf_op jit(solution)/shard_map/ppermute | solution.py:306
  15.4 0.6 collective-permute-start.4
  15.9 2.9 %whiten.1.mine_ref = bf16[2,4,48,1024]{3,2,1,0:T(8,128)(2,1)} custom-call(bf16[2,4,48,1024]{3,2,1,0:T(8,128)(2,1)} %bitcast.59, bf16[512,256]{1,0:T(8,128)(2,1)} %constant.57.clone.band_ref), custom_call_target="tpu_custom_call" | custom-call | flops 800000000 | bytes 2000000 | tf_op jit(solution)/shard_map/whiten/pallas_call | solution.py:117
  18.9 3.0 %collective-permute-start.3 = (bf16[2,4,48,1024]{3,2,1,0:T(8,128)(2,1)}, bf16[2,4,48,1024]{3,2,1,0:T(8,128)(2,1)S(1)}, u32[]{:S(2)}, u32[]{:S(2)}) collective-permute-start(bf16[2,4,48,1024]{3,2,1,0:T(8,128)(2,1)} %whiten.1.mine_ref), channel_id=1, source_target_pairs={{0,1},{1,0},{2,3},{3,2},{4,5},{5,4},{6,7},{7,6},{8,9},{9,8},{10,11... | collective-permute-start | bytes 2359304 | tf_op jit(solution)/shard_map/ppermute | solution.py:316
  21.9 0.0 collective-permute-done.6
  21.9 0.0 collective-permute-done.5
  21.9 0.0 collective-permute-done.4
  22.0 0.1 constant_dynamic-slice_fusion.4
  22.1 1.8 %collective-permute-start.7 = (bf16[2,4,2,1024]{3,1,0,2:T(4,128)(2,1)S(1)}, bf16[2,4,2,1024]{3,1,0,2:T(4,128)(2,1)S(1)}, u32[]{:S(2)}, u32[]{:S(2)}) collective-permute-start(bf16[2,4,2,1024]{3,1,0,2:T(4,128)(2,1)S(1)} %bitcast.76), channel_id=1, source_target_pairs={{0,1},{1,0},{2,3},{3,2},{4,5},{5,4},{6,7},{7,6},{8,9},{9,8},{10,11... | collective-permute-start | bytes 98312 | tf_op jit(solution)/shard_map/ppermute | solution.py:314
  23.9 0.2 broadcast_multiply_fusion
  24.0 0.1 mul.78.member_ref
  24.2 0.5 collective-permute-done.7
  24.8 0.0 collective-permute-done.3.other_ref
  24.8 0.0 copy-done.1
  24.8 0.0 copy-start
  24.8 1.1 %copy-done = bf16[2,4,48,1024]{3,2,1,0:T(8,128)(2,1)S(1)} copy-done((bf16[2,4,48,1024]{3,2,1,0:T(8,128)(2,1)S(1)}, bf16[2,4,48,1024]{3,2,1,0:T(8,128)(2,1)}, u32[]{:S(2)}) %copy-start) | copy-done | bytes 786456
  25.9 21.7 %stack.25 = bf16[16,8,3,8,256]{4,3,2,1,0:T(8,128)(2,1)} custom-call(bf16[2,4,48,1024]{3,2,1,0:T(8,128)(2,1)S(1)} %copy-done, bf16[2,4,48,1024]{3,2,1,0:T(8,128)(2,1)S(1)} %collective-permute-done.3.other_ref, bf16[32,1024]{1,0:T(8,128)(2,1)S(1)} %reshape.64.src_ref, bf16[4,1024,1024]{2,1,0:T(8,128)(2,1)} %constant.58.clone.table_ref, ...), custom_call_target="tpu_custom_call" | custom-call | flops 14000000000 | bytes 12000000 | tf_op jit(solution)/shard_map/stack/pallas_call | solution.py:260
  47.7 7.1 %all-to-all-start = ((bf16[64,6,8,256]{3,2,1,0:T(8,128)(2,1)}), bf16[64,6,8,256]{3,2,1,0:T(8,128)(2,1)S(1)}, u32[]{:S(2)}, u32[]{:S(2)}) async-start(bf16[64,6,8,256]{3,2,1,0:T(8,128)(2,1)} %bitcast.9), calls=%async_computation | async-start | bytes 3145728 | tf_op jit(solution)/shard_map/all_to_all | solution.py:329
  54.7 0.1 fusion.9
  54.8 23.5 %all-to-all-done = bf16[64,6,8,256]{3,2,1,0:T(8,128)(2,1)S(1)} async-done(((bf16[64,6,8,256]{3,2,1,0:T(8,128)(2,1)}), bf16[64,6,8,256]{3,2,1,0:T(8,128)(2,1)S(1)}, u32[]{:S(2)}, u32[]{:S(2)}) %all-to-all-start) | async-done | bytes 1572896 | tf_op jit(solution)/shard_map/all_to_all | solution.py:329
  78.4 0.2 convert_reduce_fusion
  78.6 0.1 fusion.6
  78.8 2.0 %collective-permute-start.8 = (f32[2,2,2,256]{3,2,1,0:T(2,128)S(1)}, f32[2,2,2,256]{3,2,1,0:T(2,128)S(1)}, u32[]{:S(2)}, u32[]{:S(2)}) collective-permute-start(f32[2,2,2,256]{3,2,1,0:T(2,128)S(1)} %get-tuple-element.12), channel_id=1, source_target_pairs={{0,1},{1,0},{2,3},{3,2},{4,5},{5,4},{6,7},{7,6},{8,9},{9,8},{10,11... | collective-permute-start | bytes 24584 | tf_op jit(solution)/shard_map/ppermute | solution.py:337
  80.8 0.8 %collective-permute-done.8 = f32[2,2,2,256]{3,2,1,0:T(2,128)S(1)} collective-permute-done((f32[2,2,2,256]{3,2,1,0:T(2,128)S(1)}, f32[2,2,2,256]{3,2,1,0:T(2,128)S(1)}, u32[]{:S(2)}, u32[]{:S(2)}) %collective-permute-start.8) | collective-permute-done | bytes 8224 | tf_op jit(solution)/shard_map/ppermute | solution.py:337
  81.7 0.4 rev.3
  82.1 0.6 broadcast_select_fusion
  (18 shorter events, 0.3 us)
Async XLA Ops:
  2.1 8.6 %copy-start.2 = (bf16[4,4,2,1152]{3,2,1,0:T(2,128)(2,1)S(1)}, bf16[4,4,2,1152]{3,2,1,0:T(2,128)(2,1)}, u32[]{:S(2)}) copy-start(bf16[4,4,2,1152]{3,2,1,0:T(2,128)(2,1)} %pick.1) | copy-start | bytes 221188
  2.1 8.1 %collective-permute-start.2 = (bf16[4,4,2,1152]{3,2,1,0:T(2,128)(2,1)}, bf16[4,4,2,1152]{3,2,1,0:T(2,128)(2,1)S(1)}, u32[]{:S(2)}, u32[]{:S(2)}) collective-permute-start(bf16[4,4,2,1152]{3,2,1,0:T(2,128)(2,1)} %pick.1), channel_id=1, source_target_pairs={{0,16},{1,65},{2,18},{3,67},{4,20},{5,69},{6,22},{7,71},{8,24},{9,... | collective-permute-start | bytes 221192 | tf_op jit(solution)/shard_map/ppermute | solution.py:306
  5.4 4.9 %collective-permute-start.1 = (bf16[4,4,2,1152]{3,2,1,0:T(2,128)(2,1)}, bf16[4,4,2,1152]{3,2,1,0:T(2,128)(2,1)S(1)}, u32[]{:S(2)}, u32[]{:S(2)}) collective-permute-start(bf16[4,4,2,1152]{3,2,1,0:T(2,128)(2,1)} %pick.1), channel_id=1, source_target_pairs={{0,24},{1,97},{2,26},{3,99},{4,28},{5,101},{6,30},{7,103},{8,0},{9... | collective-permute-start | bytes 221192 | tf_op jit(solution)/shard_map/ppermute | solution.py:306
  6.1 4.6 %collective-permute-start = (bf16[4,4,2,1152]{3,2,1,0:T(2,128)(2,1)}, bf16[4,4,2,1152]{3,2,1,0:T(2,128)(2,1)S(1)}, u32[]{:S(2)}, u32[]{:S(2)}) collective-permute-start(bf16[4,4,2,1152]{3,2,1,0:T(2,128)(2,1)} %pick.1), channel_id=1, source_target_pairs={{0,8},{1,33},{2,10},{3,35},{4,12},{5,37},{6,14},{7,39},{8,16},{9,4... | collective-permute-start | bytes 221192 | tf_op jit(solution)/shard_map/ppermute | solution.py:306
  10.8 14.0 %copy-start.1 = (bf16[1024,256]{1,0:T(8,128)(2,1)S(1)}, bf16[1024,256]{1,0:T(8,128)(2,1)}, u32[]{:S(2)}) copy-start(bf16[1024,256]{1,0:T(8,128)(2,1)} %constant.59.clone.edge_table_ref) | copy-start | bytes 1572868
  10.8 11.1 %collective-permute-start.6 = (bf16[4,4,2,1152]{3,2,1,0:T(2,128)(2,1)S(1)}, bf16[4,4,2,1152]{3,2,1,0:T(2,128)(2,1)S(1)}, u32[]{:S(2)}, u32[]{:S(2)}) collective-permute-start(bf16[4,4,2,1152]{3,2,1,0:T(2,128)(2,1)S(1)} %bitcast.61), channel_id=1, source_target_pairs={{0,64},{1,17},{2,66},{3,19},{4,68},{5,21},{6,70},{7,23},{8,72},{9,... | collective-permute-start | bytes 221192 | tf_op jit(solution)/shard_map/ppermute | solution.py:306
  14.5 7.4 %collective-permute-start.5 = (bf16[4,4,2,1152]{3,2,1,0:T(2,128)(2,1)S(1)}, bf16[4,4,2,1152]{3,2,1,0:T(2,128)(2,1)S(1)}, u32[]{:S(2)}, u32[]{:S(2)}) collective-permute-start(bf16[4,4,2,1152]{3,2,1,0:T(2,128)(2,1)S(1)} %bitcast.62), channel_id=1, source_target_pairs={{0,96},{1,25},{2,98},{3,27},{4,100},{5,29},{6,102},{7,31},{8,104},... | collective-permute-start | bytes 221192 | tf_op jit(solution)/shard_map/ppermute | solution.py:306
  15.4 6.5 %collective-permute-start.4 = (bf16[4,4,2,1152]{3,2,1,0:T(2,128)(2,1)S(1)}, bf16[4,4,2,1152]{3,2,1,0:T(2,128)(2,1)S(1)}, u32[]{:S(2)}, u32[]{:S(2)}) collective-permute-start(bf16[4,4,2,1152]{3,2,1,0:T(2,128)(2,1)S(1)} %bitcast.63), channel_id=1, source_target_pairs={{0,32},{1,9},{2,34},{3,11},{4,36},{5,13},{6,38},{7,15},{8,40},{9,1... | collective-permute-start | bytes 221192 | tf_op jit(solution)/shard_map/ppermute | solution.py:306
  18.9 5.9 %collective-permute-start.3 = (bf16[2,4,48,1024]{3,2,1,0:T(8,128)(2,1)}, bf16[2,4,48,1024]{3,2,1,0:T(8,128)(2,1)S(1)}, u32[]{:S(2)}, u32[]{:S(2)}) collective-permute-start(bf16[2,4,48,1024]{3,2,1,0:T(8,128)(2,1)} %whiten.1.mine_ref), channel_id=1, source_target_pairs={{0,1},{1,0},{2,3},{3,2},{4,5},{5,4},{6,7},{7,6},{8,9},{9,8},{10,11... | collective-permute-start | bytes 2359304 | tf_op jit(solution)/shard_map/ppermute | solution.py:316
  22.1 2.6 %collective-permute-start.7 = (bf16[2,4,2,1024]{3,1,0,2:T(4,128)(2,1)S(1)}, bf16[2,4,2,1024]{3,1,0,2:T(4,128)(2,1)S(1)}, u32[]{:S(2)}, u32[]{:S(2)}) collective-permute-start(bf16[2,4,2,1024]{3,1,0,2:T(4,128)(2,1)S(1)} %bitcast.76), channel_id=1, source_target_pairs={{0,1},{1,0},{2,3},{3,2},{4,5},{5,4},{6,7},{7,6},{8,9},{9,8},{10,11... | collective-permute-start | bytes 98312 | tf_op jit(solution)/shard_map/ppermute | solution.py:314
  24.8 1.1 %copy-start = (bf16[2,4,48,1024]{3,2,1,0:T(8,128)(2,1)S(1)}, bf16[2,4,48,1024]{3,2,1,0:T(8,128)(2,1)}, u32[]{:S(2)}) copy-start(bf16[2,4,48,1024]{3,2,1,0:T(8,128)(2,1)} %whiten.1.mine_ref) | copy-start | bytes 2359300
  47.7 30.7 %all-to-all-start = ((bf16[64,6,8,256]{3,2,1,0:T(8,128)(2,1)}), bf16[64,6,8,256]{3,2,1,0:T(8,128)(2,1)S(1)}, u32[]{:S(2)}, u32[]{:S(2)}) async-start(bf16[64,6,8,256]{3,2,1,0:T(8,128)(2,1)} %bitcast.9), calls=%async_computation | async-start | bytes 3145728 | tf_op jit(solution)/shard_map/all_to_all | solution.py:329
  78.8 2.9 %collective-permute-start.8 = (f32[2,2,2,256]{3,2,1,0:T(2,128)S(1)}, f32[2,2,2,256]{3,2,1,0:T(2,128)S(1)}, u32[]{:S(2)}, u32[]{:S(2)}) collective-permute-start(f32[2,2,2,256]{3,2,1,0:T(2,128)S(1)} %get-tuple-element.12), channel_id=1, source_target_pairs={{0,1},{1,0},{2,3},{3,2},{4,5},{5,4},{6,7},{7,6},{8,9},{9,8},{10,11... | collective-permute-start | bytes 24584 | tf_op jit(solution)/shard_map/ppermute | solution.py:337

commit v4 on v3

--- a/solution.py
+++ b/solution.py
@@ -127,7 +127,7 @@
 
 def stack_kernel(
     mine_ref, other_ref, src_ref, table_ref, edge_table_ref, member_ref, out_ref,
-    src_sc, cross_sc, prod_sc, edge_prod_sc, minus_sc, edge_sc, sums_sc, table_sc, table_sem, part_sc, part_sem,
+    src_sc, cross_sc, prod_sc, edge_prod_sc, minus_sc, plus_sc, edge_sc, sums_sc, table_sc, table_sem, part_sc, part_sem, out_sc, out_sem,
 ):
     step_id = pl.program_id(0)
     block = PAIRS - 1 - step_id
@@ -136,6 +136,10 @@
 
     def fetch(step):
         return pltpu.make_async_copy(table_ref.at[PAIRS - 1 - step], table_sc.at[step % 2], table_sem.at[step % 2])
+
+    def leave(done, sign):
+        win = PAIRS - 1 - done if sign else PAIRS + done
+        return pltpu.make_async_copy(out_sc.at[:, win], out_ref.at[:, win], out_sem.at[done, sign])
 
     parts = [
         pltpu.make_async_copy(ref, part_sc.at[i], part_sem.at[i])
@@ -205,29 +209,29 @@
     def epilogue(i):
         h, s = divmod(i, 2)
         slot = i % 2
-        for g in range(3):
+        for g in range(6):
             for t in range(2):
-                zero = jnp.zeros((16, 128), f32)
+                zero = jnp.zeros((8, 128), f32)
                 sa, sb, pr, pi, mr, mi = (zero,) * 6
                 for w in range(8):
-                    at = w * 48 + 16 * g
+                    at = w * 48 + 8 * g
                     lo = slice(128 * t, 128 * t + 128)
                     hi = slice(256 + 128 * t, 256 + 128 * t + 128)
-                    a = prod_sc[slot, at : at + 16, lo]
-                    d = prod_sc[slot, at : at + 16, hi]
-                    c = prod_sc[slot, 384 + at : 384 + at + 16, lo]
-                    b = prod_sc[slot, 384 + at : 384 + at + 16, hi]
+                    a = prod_sc[slot, at : at + 8, lo]
+                    d = prod_sc[slot, at : at + 8, hi]
+                    c = prod_sc[slot, 384 + at : 384 + at + 8, lo]
+                    b = prod_sc[slot, 384 + at : 384 + at + 8, hi]
                     sa, sb = sa + a, sb + b
                     ur, ui = unit(a - b, c + d)
                     pr, pi = pr + ur, pi + ui
                     ur, ui = unit(a + b, c - d)
                     mr, mi = mr + ur, mi + ui
-                at = h * 96 + s * 48 + 16 * g
+                at = h * 96 + s * 48 + 8 * g
                 for k, value in enumerate((sa - sb, pr, pi)):
-                    sums_sc[0, k, at : at + 16, 128 * t : 128 * t + 128] = value.astype(bf16)
+                    plus_sc[k, at : at + 8, 128 * t : 128 * t + 128] = value
                 for k, value in enumerate((sa + sb, mr, mi)):
                     lo = 256 * h + 128 * t
-                    minus_sc[k, s, 16 * g : 16 * g + 16, lo : lo + 128] = value
+                    minus_sc[k, s, 8 * g : 8 * g + 8, lo : lo + 128] = value
 
     fetch(step_id).wait()
     product(0)
@@ -249,8 +253,16 @@
     for sign in range(2):
         win = PAIRS - 1 - block if sign else PAIRS + block
         for k in range(3):
-            binned = jnp.dot(member_ref[...], sums_sc[sign, k], preferred_element_type=f32)
-            out_ref[:, win, k] = binned.reshape(16, 8, HALF).astype(bf16)
+            sums = sums_sc[1, k] if sign else plus_sc[k].astype(bf16)
+            binned = jnp.dot(member_ref[...], sums, preferred_element_type=f32)
+            out_sc[:, win, k] = binned.reshape(16, 8, HALF).astype(bf16)
+        leave(block, sign).start()
+
+    @pl.when(step_id == PAIRS - 1)
+    def _():
+        for done in range(PAIRS):
+            for sign in range(2):
+                leave(done, sign).wait()
 
 
 def stack_partial(parts, src, member):
@@ -260,8 +272,8 @@
     return pl.pallas_call(
         stack_kernel,
         grid=(PAIRS,),
-        in_specs=[hbm, hbm, vmem, hbm, vmem, vmem],
-        out_specs=vmem,
+        in_specs=[pl.BlockSpec(memory_space=pltpu.HBM)] * 2 + [vmem, hbm, vmem, vmem],
+        out_specs=hbm,
         out_shape=jax.ShapeDtypeStruct((16, 8, 3, 8, HALF), bf16),
         scratch_shapes=[
             pltpu.VMEM((2, 16, F), f32),
@@ -269,12 +281,15 @@
             pltpu.VMEM((2, 768, 512), f32),
             pltpu.VMEM((768, 256), f32),
             pltpu.VMEM((3, 2, 48, BLOCK), f32),
+            pltpu.VMEM((3, 192, HALF), f32),
             pltpu.VMEM((3, 2, 48, 128), f32),
             pltpu.VMEM((2, 3, 192, HALF), bf16),
             pltpu.VMEM((2, F, 1024), bf16),
             pltpu.SemaphoreType.DMA((2,)),
             pltpu.VMEM((2, 2, 4, 48, F), bf16),
             pltpu.SemaphoreType.DMA((2,)),
+            pltpu.VMEM((16, 8, 3, 8, HALF), bf16),
+            pltpu.SemaphoreType.DMA((PAIRS, 2)),
         ],
         compiler_params=pltpu.CompilerParams(vmem_limit_bytes=48 << 20),
         cost_estimate=pl.CostEstimate(flops=14 * 10**9, bytes_accessed=12 * 10**6, transcendentals=6 * 10**6),

time: 82.8 us -> 81.5 us (0.984)
  Pallas kernels: 26.7 us -> 25.8 us
    pallas_call x1, Pallas kernels: 21.7 us -> 20.7 us  [stack_partial(): pl.pallas_call(stack_kernel, grid=(PAIRS,), in_specs=[pl.BlockSpec(memory...]
where the time goes in v4:
time: 81.5 us; the launch traced here: 81.1 us
  Pallas kernels  25.8 us (32%)
  waiting for transfers between devices  25.6 us (31%)
  starting transfers between devices  22.9 us (28%)
  local copies, waits for them, and re-layouts  5.03 us (6%)
  other arithmetic  1.53 us (2%)
    all_to_all x1, waiting for transfers between devices, shards(): lax.all_to_all(partial.reshape(64, 6, 8, HALF), ('y', 'z', 'x'), 0, 0, ti...  23.7 us
    pallas_call x1, Pallas kernels, stack_partial(): pl.pallas_call(stack_kernel, grid=(PAIRS,), in_specs=[pl.BlockSpec(memory...  20.7 us
    ppermute x6, starting transfers between devices, shards(): lax.ppermute(sent, ('y', 'z', 'x', 'c'), crossed(k, stage))  9.78 us
    all_to_all x1, starting transfers between devices, shards(): lax.all_to_all(partial.reshape(64, 6, 8, HALF), ('y', 'z', 'x'), 0, 0, ti...  6.63 us
    unnamed x8, local copies, waits for them, and re-layouts  3.6 us
    pallas_call x1, Pallas kernels, whiten(): pl.pallas_call(whiten_kernel, in_specs=[vmem, vmem], out_specs=vmem, out_...  2.91 us
    ppermute x1, starting transfers between devices, shards(): parts = [mine, lax.ppermute(mine, 'c', swap)]  2.88 us
    pallas_call x1, Pallas kernels, pick(): pl.pallas_call(pick_kernel, in_specs=[pl.BlockSpec(memory_space=pltpu.SME...  2.17 us
  transfers between devices with their start and end apart: 10, of which 4 were waited for; matrix products, arithmetic and copies ran while one was open for 5% of the time, Pallas kernels for 4%

profile of v4, /device:TPU:1, one launch (start us, length us, event | category | flops | bytes accessed | tf_op | source)
XLA Modules:
  0.0 81.1 jit_solution(4998372684790890825)
XLA Ops:
  0.0 2.2 %pick.1 = bf16[4,4,2,1152]{3,2,1,0:T(2,128)(2,1)} custom-call(s32[4]{0:T(128)} %sources_ref.1, s32[4,3,1,32]{3,2,1,0:T(1,128)} %bitcast.78, bf16[48,4,2,1024]{3,2,1,0:T(2,128)(2,1)} %spectra_ref.1), custom_call_target="tpu_custom_call" | custom-call | tf_op jit(solution)/shard_map/pick/pallas_call | solution.py:79
  2.2 0.0 copy-start.2
  2.2 3.2 %collective-permute-start.2 = (bf16[4,4,2,1152]{3,2,1,0:T(2,128)(2,1)}, bf16[4,4,2,1152]{3,2,1,0:T(2,128)(2,1)S(1)}, u32[]{:S(2)}, u32[]{:S(2)}) collective-permute-start(bf16[4,4,2,1152]{3,2,1,0:T(2,128)(2,1)} %pick.1), channel_id=1, source_target_pairs={{0,16},{1,65},{2,18},{3,67},{4,20},{5,69},{6,22},{7,71},{8,24},{9,... | collective-permute-start | bytes 221192 | tf_op jit(solution)/shard_map/ppermute | solution.py:321
  5.4 0.8 collective-permute-start.1
  6.1 0.7 collective-permute-start
  6.8 0.7 constant_dynamic-slice_fusion.2
  7.5 0.1 fusion
  7.6 0.1 broadcast_multiply_fusion.1
  7.8 2.4 %copy.40 = bf16[48,4,2,1024]{3,0,1,2:T(8,128)(2,1)} copy(bf16[48,4,2,1024]{3,2,1,0:T(2,128)(2,1)} %spectra_ref.1) | data formatting | bytes 1572864 | tf_op args[0]
  10.2 0.0 collective-permute-done.2
  10.2 0.0 collective-permute-done.1
  10.2 0.5 collective-permute-done
  10.8 0.0 copy-done.2
  10.8 0.0 copy-start.1
  10.8 3.7 %collective-permute-start.6 = (bf16[4,4,2,1152]{3,2,1,0:T(2,128)(2,1)S(1)}, bf16[4,4,2,1152]{3,2,1,0:T(2,128)(2,1)S(1)}, u32[]{:S(2)}, u32[]{:S(2)}) collective-permute-start(bf16[4,4,2,1152]{3,2,1,0:T(2,128)(2,1)S(1)} %bitcast.61), channel_id=1, source_target_pairs={{0,64},{1,17},{2,66},{3,19},{4,68},{5,21},{6,70},{7,23},{8,72},{9,... | collective-permute-start | bytes 221192 | tf_op jit(solution)/shard_map/ppermute | solution.py:321
  14.5 0.4 collective-permute-start.5
  14.9 1.0 %collective-permute-start.4 = (bf16[4,4,2,1152]{3,2,1,0:T(2,128)(2,1)S(1)}, bf16[4,4,2,1152]{3,2,1,0:T(2,128)(2,1)S(1)}, u32[]{:S(2)}, u32[]{:S(2)}) collective-permute-start(bf16[4,4,2,1152]{3,2,1,0:T(2,128)(2,1)S(1)} %bitcast.63), channel_id=1, source_target_pairs={{0,32},{1,9},{2,34},{3,11},{4,36},{5,13},{6,38},{7,15},{8,40},{9,1... | collective-permute-start | bytes 221192 | tf_op jit(solution)/shard_map/ppermute | solution.py:321
  15.9 2.9 %whiten.1.mine_ref = bf16[2,4,48,1024]{3,2,1,0:T(8,128)(2,1)} custom-call(bf16[2,4,48,1024]{3,2,1,0:T(8,128)(2,1)} %bitcast.59, bf16[512,256]{1,0:T(8,128)(2,1)} %constant.57.clone.band_ref), custom_call_target="tpu_custom_call" | custom-call | flops 800000000 | bytes 2000000 | tf_op jit(solution)/shard_map/whiten/pallas_call | solution.py:117
  18.9 2.9 %collective-permute-start.3 = (bf16[2,4,48,1024]{3,2,1,0:T(8,128)(2,1)}, bf16[2,4,48,1024]{3,2,1,0:T(8,128)(2,1)S(1)}, u32[]{:S(2)}, u32[]{:S(2)}) collective-permute-start(bf16[2,4,48,1024]{3,2,1,0:T(8,128)(2,1)} %whiten.1.mine_ref), channel_id=1, source_target_pairs={{0,1},{1,0},{2,3},{3,2},{4,5},{5,4},{6,7},{7,6},{8,9},{9,8},{10,11... | collective-permute-start | bytes 2359304 | tf_op jit(solution)/shard_map/ppermute | solution.py:331
  21.7 0.0 collective-permute-done.6
  21.7 0.0 collective-permute-done.5
  21.7 0.0 collective-permute-done.4
  21.8 0.1 constant_dynamic-slice_fusion.4
  21.9 1.8 %collective-permute-start.7 = (bf16[2,4,2,1024]{3,1,0,2:T(4,128)(2,1)S(1)}, bf16[2,4,2,1024]{3,1,0,2:T(4,128)(2,1)S(1)}, u32[]{:S(2)}, u32[]{:S(2)}) collective-permute-start(bf16[2,4,2,1024]{3,1,0,2:T(4,128)(2,1)S(1)} %bitcast.76), channel_id=1, source_target_pairs={{0,1},{1,0},{2,3},{3,2},{4,5},{5,4},{6,7},{7,6},{8,9},{9,8},{10,11... | collective-permute-start | bytes 98312 | tf_op jit(solution)/shard_map/ppermute | solution.py:329
  23.7 0.2 broadcast_multiply_fusion
  23.8 0.1 mul.78.member_ref
  24.0 0.5 collective-permute-done.7
  24.6 0.0 collective-permute-done.3.other_ref
  24.6 0.0 copy-done.1
  24.6 0.0 copy-start
  24.6 1.1 %copy-done = bf16[2,4,48,1024]{3,2,1,0:T(8,128)(2,1)S(1)} copy-done((bf16[2,4,48,1024]{3,2,1,0:T(8,128)(2,1)S(1)}, bf16[2,4,48,1024]{3,2,1,0:T(8,128)(2,1)}, u32[]{:S(2)}) %copy-start) | copy-done | bytes 786456
  25.8 20.7 %stack.25 = bf16[16,8,3,8,256]{4,3,2,1,0:T(8,128)(2,1)} custom-call(bf16[2,4,48,1024]{3,2,1,0:T(8,128)(2,1)S(1)} %copy-done, bf16[2,4,48,1024]{3,2,1,0:T(8,128)(2,1)S(1)} %collective-permute-done.3.other_ref, bf16[32,1024]{1,0:T(8,128)(2,1)S(1)} %reshape.64.src_ref, bf16[4,1024,1024]{2,1,0:T(8,128)(2,1)} %constant.58.clone.table_ref, ...), custom_call_target="tpu_custom_call" | custom-call | flops 14000000000 | bytes 12000000 | tf_op jit(solution)/shard_map/stack/pallas_call | solution.py:272
  46.4 6.6 %all-to-all-start = ((bf16[64,6,8,256]{3,2,1,0:T(8,128)(2,1)}), bf16[64,6,8,256]{3,2,1,0:T(8,128)(2,1)S(1)}, u32[]{:S(2)}, u32[]{:S(2)}) async-start(bf16[64,6,8,256]{3,2,1,0:T(8,128)(2,1)} %bitcast.9), calls=%async_computation | async-start | bytes 3145728 | tf_op jit(solution)/shard_map/all_to_all | solution.py:344
  53.1 0.1 fusion.9
  53.2 23.7 %all-to-all-done = bf16[64,6,8,256]{3,2,1,0:T(8,128)(2,1)S(1)} async-done(((bf16[64,6,8,256]{3,2,1,0:T(8,128)(2,1)}), bf16[64,6,8,256]{3,2,1,0:T(8,128)(2,1)S(1)}, u32[]{:S(2)}, u32[]{:S(2)}) %all-to-all-start) | async-done | bytes 1572896 | tf_op jit(solution)/shard_map/all_to_all | solution.py:344
  76.9 0.2 convert_reduce_fusion
  77.2 0.1 fusion.6
  77.3 1.9 %collective-permute-start.8 = (f32[2,2,2,256]{3,2,1,0:T(2,128)S(1)}, f32[2,2,2,256]{3,2,1,0:T(2,128)S(1)}, u32[]{:S(2)}, u32[]{:S(2)}) collective-permute-start(f32[2,2,2,256]{3,2,1,0:T(2,128)S(1)} %get-tuple-element.12), channel_id=1, source_target_pairs={{0,1},{1,0},{2,3},{3,2},{4,5},{5,4},{6,7},{7,6},{8,9},{9,8},{10,11... | collective-permute-start | bytes 24584 | tf_op jit(solution)/shard_map/ppermute | solution.py:352
  79.2 0.8 %collective-permute-done.8 = f32[2,2,2,256]{3,2,1,0:T(2,128)S(1)} collective-permute-done((f32[2,2,2,256]{3,2,1,0:T(2,128)S(1)}, f32[2,2,2,256]{3,2,1,0:T(2,128)S(1)}, u32[]{:S(2)}, u32[]{:S(2)}) %collective-permute-start.8) | collective-permute-done | bytes 8224 | tf_op jit(solution)/shard_map/ppermute | solution.py:352
  80.1 0.4 rev.3
  80.5 0.6 broadcast_select_fusion
  (18 shorter events, 0.3 us)
Async XLA Ops:
  2.2 8.6 %copy-start.2 = (bf16[4,4,2,1152]{3,2,1,0:T(2,128)(2,1)S(1)}, bf16[4,4,2,1152]{3,2,1,0:T(2,128)(2,1)}, u32[]{:S(2)}) copy-start(bf16[4,4,2,1152]{3,2,1,0:T(2,128)(2,1)} %pick.1) | copy-start | bytes 221188
  2.2 8.0 %collective-permute-start.2 = (bf16[4,4,2,1152]{3,2,1,0:T(2,128)(2,1)}, bf16[4,4,2,1152]{3,2,1,0:T(2,128)(2,1)S(1)}, u32[]{:S(2)}, u32[]{:S(2)}) collective-permute-start(bf16[4,4,2,1152]{3,2,1,0:T(2,128)(2,1)} %pick.1), channel_id=1, source_target_pairs={{0,16},{1,65},{2,18},{3,67},{4,20},{5,69},{6,22},{7,71},{8,24},{9,... | collective-permute-start | bytes 221192 | tf_op jit(solution)/shard_map/ppermute | solution.py:321
  5.4 4.9 %collective-permute-start.1 = (bf16[4,4,2,1152]{3,2,1,0:T(2,128)(2,1)}, bf16[4,4,2,1152]{3,2,1,0:T(2,128)(2,1)S(1)}, u32[]{:S(2)}, u32[]{:S(2)}) collective-permute-start(bf16[4,4,2,1152]{3,2,1,0:T(2,128)(2,1)} %pick.1), channel_id=1, source_target_pairs={{0,24},{1,97},{2,26},{3,99},{4,28},{5,101},{6,30},{7,103},{8,0},{9... | collective-permute-start | bytes 221192 | tf_op jit(solution)/shard_map/ppermute | solution.py:321
  6.1 4.6 %collective-permute-start = (bf16[4,4,2,1152]{3,2,1,0:T(2,128)(2,1)}, bf16[4,4,2,1152]{3,2,1,0:T(2,128)(2,1)S(1)}, u32[]{:S(2)}, u32[]{:S(2)}) collective-permute-start(bf16[4,4,2,1152]{3,2,1,0:T(2,128)(2,1)} %pick.1), channel_id=1, source_target_pairs={{0,8},{1,33},{2,10},{3,35},{4,12},{5,37},{6,14},{7,39},{8,16},{9,4... | collective-permute-start | bytes 221192 | tf_op jit(solution)/shard_map/ppermute | solution.py:321
  10.8 13.8 %copy-start.1 = (bf16[1024,256]{1,0:T(8,128)(2,1)S(1)}, bf16[1024,256]{1,0:T(8,128)(2,1)}, u32[]{:S(2)}) copy-start(bf16[1024,256]{1,0:T(8,128)(2,1)} %constant.59.clone.edge_table_ref) | copy-start | bytes 1572868
  10.8 10.9 %collective-permute-start.6 = (bf16[4,4,2,1152]{3,2,1,0:T(2,128)(2,1)S(1)}, bf16[4,4,2,1152]{3,2,1,0:T(2,128)(2,1)S(1)}, u32[]{:S(2)}, u32[]{:S(2)}) collective-permute-start(bf16[4,4,2,1152]{3,2,1,0:T(2,128)(2,1)S(1)} %bitcast.61), channel_id=1, source_target_pairs={{0,64},{1,17},{2,66},{3,19},{4,68},{5,21},{6,70},{7,23},{8,72},{9,... | collective-permute-start | bytes 221192 | tf_op jit(solution)/shard_map/ppermute | solution.py:321
  14.5 7.3 %collective-permute-start.5 = (bf16[4,4,2,1152]{3,2,1,0:T(2,128)(2,1)S(1)}, bf16[4,4,2,1152]{3,2,1,0:T(2,128)(2,1)S(1)}, u32[]{:S(2)}, u32[]{:S(2)}) collective-permute-start(bf16[4,4,2,1152]{3,2,1,0:T(2,128)(2,1)S(1)} %bitcast.62), channel_id=1, source_target_pairs={{0,96},{1,25},{2,98},{3,27},{4,100},{5,29},{6,102},{7,31},{8,104},... | collective-permute-start | bytes 221192 | tf_op jit(solution)/shard_map/ppermute | solution.py:321
  14.9 6.8 %collective-permute-start.4 = (bf16[4,4,2,1152]{3,2,1,0:T(2,128)(2,1)S(1)}, bf16[4,4,2,1152]{3,2,1,0:T(2,128)(2,1)S(1)}, u32[]{:S(2)}, u32[]{:S(2)}) collective-permute-start(bf16[4,4,2,1152]{3,2,1,0:T(2,128)(2,1)S(1)} %bitcast.63), channel_id=1, source_target_pairs={{0,32},{1,9},{2,34},{3,11},{4,36},{5,13},{6,38},{7,15},{8,40},{9,1... | collective-permute-start | bytes 221192 | tf_op jit(solution)/shard_map/ppermute | solution.py:321
  18.9 5.8 %collective-permute-start.3 = (bf16[2,4,48,1024]{3,2,1,0:T(8,128)(2,1)}, bf16[2,4,48,1024]{3,2,1,0:T(8,128)(2,1)S(1)}, u32[]{:S(2)}, u32[]{:S(2)}) collective-permute-start(bf16[2,4,48,1024]{3,2,1,0:T(8,128)(2,1)} %whiten.1.mine_ref), channel_id=1, source_target_pairs={{0,1},{1,0},{2,3},{3,2},{4,5},{5,4},{6,7},{7,6},{8,9},{9,8},{10,11... | collective-permute-start | bytes 2359304 | tf_op jit(solution)/shard_map/ppermute | solution.py:331
  21.9 2.6 %collective-permute-start.7 = (bf16[2,4,2,1024]{3,1,0,2:T(4,128)(2,1)S(1)}, bf16[2,4,2,1024]{3,1,0,2:T(4,128)(2,1)S(1)}, u32[]{:S(2)}, u32[]{:S(2)}) collective-permute-start(bf16[2,4,2,1024]{3,1,0,2:T(4,128)(2,1)S(1)} %bitcast.76), channel_id=1, source_target_pairs={{0,1},{1,0},{2,3},{3,2},{4,5},{5,4},{6,7},{7,6},{8,9},{9,8},{10,11... | collective-permute-start | bytes 98312 | tf_op jit(solution)/shard_map/ppermute | solution.py:329
  24.6 1.1 %copy-start = (bf16[2,4,48,1024]{3,2,1,0:T(8,128)(2,1)S(1)}, bf16[2,4,48,1024]{3,2,1,0:T(8,128)(2,1)}, u32[]{:S(2)}) copy-start(bf16[2,4,48,1024]{3,2,1,0:T(8,128)(2,1)} %whiten.1.mine_ref) | copy-start | bytes 2359300
  46.4 30.5 %all-to-all-start = ((bf16[64,6,8,256]{3,2,1,0:T(8,128)(2,1)}), bf16[64,6,8,256]{3,2,1,0:T(8,128)(2,1)S(1)}, u32[]{:S(2)}, u32[]{:S(2)}) async-start(bf16[64,6,8,256]{3,2,1,0:T(8,128)(2,1)} %bitcast.9), calls=%async_computation | async-start | bytes 3145728 | tf_op jit(solution)/shard_map/all_to_all | solution.py:344
  77.3 2.7 %collective-permute-start.8 = (f32[2,2,2,256]{3,2,1,0:T(2,128)S(1)}, f32[2,2,2,256]{3,2,1,0:T(2,128)S(1)}, u32[]{:S(2)}, u32[]{:S(2)}) collective-permute-start(f32[2,2,2,256]{3,2,1,0:T(2,128)S(1)} %get-tuple-element.12), channel_id=1, source_target_pairs={{0,1},{1,0},{2,3},{3,2},{4,5},{5,4},{6,7},{7,6},{8,9},{9,8},{10,11... | collective-permute-start | bytes 24584 | tf_op jit(solution)/shard_map/ppermute | solution.py:352

commit v5 on v4

--- a/solution.py
+++ b/solution.py
@@ -118,7 +118,7 @@
         whiten_kernel,
         in_specs=[vmem, vmem],
         out_specs=vmem,
-        out_shape=jax.ShapeDtypeStruct(x.shape, bf16),
+        out_shape=pltpu.VMEM(x.shape, bf16),
         scratch_shapes=[pltpu.VMEM((384, F + 256), bf16)],
         cost_estimate=pl.CostEstimate(flops=8 * 10**8, bytes_accessed=2 * 10**6, transcendentals=4 * 10**5),
         name="whiten",
@@ -272,7 +272,7 @@
     return pl.pallas_call(
         stack_kernel,
         grid=(PAIRS,),
-        in_specs=[pl.BlockSpec(memory_space=pltpu.HBM)] * 2 + [vmem, hbm, vmem, vmem],
+        in_specs=[hbm, hbm, vmem, hbm, vmem, vmem],
         out_specs=hbm,
         out_shape=jax.ShapeDtypeStruct((16, 8, 3, 8, HALF), bf16),
         scratch_shapes=[

time: 81.5 us -> 79.9 us (0.980)
  local copies, waits for them, and re-layouts: 5.03 us -> 3.91 us
  Pallas kernels: 25.8 us -> 24.9 us
    ppermute x1, starting transfers between devices: 1.75 us -> 3.2 us  [shards(): lax.ppermute(lax.dynamic_index_in_dim(src, 1 - c, 0, keepdims=False), 'c'...]
    unnamed x8 -> x6, local copies, waits for them, and re-layouts: 3.6 us -> 2.48 us
    all_to_all x1, starting transfers between devices: 6.63 us -> 5.58 us  [shards(): lax.all_to_all(partial.reshape(64, 6, 8, HALF), ('y', 'z', 'x'), 0, 0, ti...]
    pallas_call x1, Pallas kernels: 2.91 us -> 2 us  [whiten(): pl.pallas_call(whiten_kernel, in_specs=[vmem, vmem], out_specs=vmem, out_...]
  transfers between devices with their start and end apart: 10 -> 10, of which waited for: 4 -> 4; matrix products, arithmetic and copies ran while one was open for 5% -> 5% of each run, Pallas kernels for 4% -> 3%
where the time goes in v5:
time: 79.9 us; the launch traced here: 79.5 us
  waiting for transfers between devices  25.5 us (32%)
  Pallas kernels  24.9 us (31%)
  starting transfers between devices  23.5 us (29%)
  local copies, waits for them, and re-layouts  3.91 us (5%)
  other arithmetic  1.53 us (2%)
    all_to_all x1, waiting for transfers between devices, shards(): lax.all_to_all(partial.reshape(64, 6, 8, HALF), ('y', 'z', 'x'), 0, 0, ti...  23.6 us
    pallas_call x1, Pallas kernels, stack_partial(): pl.pallas_call(stack_kernel, grid=(PAIRS,), in_specs=[hbm, hbm, vmem, hbm...  20.7 us
    ppermute x6, starting transfers between devices, shards(): lax.ppermute(sent, ('y', 'z', 'x', 'c'), crossed(k, stage))  10.4 us
    all_to_all x1, starting transfers between devices, shards(): lax.all_to_all(partial.reshape(64, 6, 8, HALF), ('y', 'z', 'x'), 0, 0, ti...  5.58 us
    ppermute x1, starting transfers between devices, shards(): lax.ppermute(lax.dynamic_index_in_dim(src, 1 - c, 0, keepdims=False), 'c'...  3.2 us
    unnamed x6, local copies, waits for them, and re-layouts  2.48 us
    ppermute x1, starting transfers between devices, shards(): parts = [mine, lax.ppermute(mine, 'c', swap)]  2.31 us
    pallas_call x1, Pallas kernels, pick(): pl.pallas_call(pick_kernel, in_specs=[pl.BlockSpec(memory_space=pltpu.SME...  2.16 us
  transfers between devices with their start and end apart: 10, of which 4 were waited for; matrix products, arithmetic and copies ran while one was open for 5% of the time, Pallas kernels for 3%

profile of v5, /device:TPU:1, one launch (start us, length us, event | category | flops | bytes accessed | tf_op | source)
XLA Modules:
  0.0 79.5 jit_solution(15203668069787366067)
XLA Ops:
  0.0 2.2 %pick.1 = bf16[4,4,2,1152]{3,2,1,0:T(2,128)(2,1)} custom-call(s32[4]{0:T(128)} %sources_ref.1, s32[4,3,1,32]{3,2,1,0:T(1,128)} %bitcast.78, bf16[48,4,2,1024]{3,2,1,0:T(2,128)(2,1)} %spectra_ref.1), custom_call_target="tpu_custom_call" | custom-call | tf_op jit(solution)/shard_map/pick/pallas_call | solution.py:79
  2.2 0.0 copy-start.1
  2.2 3.2 %collective-permute-start.2 = (bf16[4,4,2,1152]{3,2,1,0:T(2,128)(2,1)}, bf16[4,4,2,1152]{3,2,1,0:T(2,128)(2,1)S(1)}, u32[]{:S(2)}, u32[]{:S(2)}) collective-permute-start(bf16[4,4,2,1152]{3,2,1,0:T(2,128)(2,1)} %pick.1), channel_id=1, source_target_pairs={{0,16},{1,65},{2,18},{3,67},{4,20},{5,69},{6,22},{7,71},{8,24},{9,... | collective-permute-start | bytes 221192 | tf_op jit(solution)/shard_map/ppermute | solution.py:321
  5.3 0.8 collective-permute-start.1
  6.1 0.7 collective-permute-start
  6.8 0.7 constant_dynamic-slice_fusion.2
  7.5 0.1 fusion
  7.6 0.1 broadcast_multiply_fusion.1
  7.8 2.5 %copy.40 = bf16[48,4,2,1024]{3,0,1,2:T(8,128)(2,1)} copy(bf16[48,4,2,1024]{3,2,1,0:T(2,128)(2,1)} %spectra_ref.1) | data formatting | bytes 1572864 | tf_op args[0]
  10.2 0.0 collective-permute-done.2
  10.2 0.0 collective-permute-done.1
  10.2 0.5 collective-permute-done
  10.7 0.0 copy-done.1
  10.8 0.0 copy-start
  10.8 4.3 %collective-permute-start.6 = (bf16[4,4,2,1152]{3,2,1,0:T(2,128)(2,1)S(1)}, bf16[4,4,2,1152]{3,2,1,0:T(2,128)(2,1)S(1)}, u32[]{:S(2)}, u32[]{:S(2)}) collective-permute-start(bf16[4,4,2,1152]{3,2,1,0:T(2,128)(2,1)S(1)} %bitcast.61), channel_id=1, source_target_pairs={{0,64},{1,17},{2,66},{3,19},{4,68},{5,21},{6,70},{7,23},{8,72},{9,... | collective-permute-start | bytes 221192 | tf_op jit(solution)/shard_map/ppermute | solution.py:321
  15.1 0.4 collective-permute-start.5
  15.5 1.1 %collective-permute-start.4 = (bf16[4,4,2,1152]{3,2,1,0:T(2,128)(2,1)S(1)}, bf16[4,4,2,1152]{3,2,1,0:T(2,128)(2,1)S(1)}, u32[]{:S(2)}, u32[]{:S(2)}) collective-permute-start(bf16[4,4,2,1152]{3,2,1,0:T(2,128)(2,1)S(1)} %bitcast.63), channel_id=1, source_target_pairs={{0,32},{1,9},{2,34},{3,11},{4,36},{5,13},{6,38},{7,15},{8,40},{9,1... | collective-permute-start | bytes 221192 | tf_op jit(solution)/shard_map/ppermute | solution.py:321
  16.6 2.0 %whiten.1.mine_ref = bf16[2,4,48,1024]{3,2,1,0:T(8,128)(2,1)S(1)} custom-call(bf16[2,4,48,1024]{3,2,1,0:T(8,128)(2,1)} %bitcast.59, bf16[512,256]{1,0:T(8,128)(2,1)} %constant.57.clone.band_ref), custom_call_target="tpu_custom_call" | custom-call | flops 800000000 | bytes 2000000 | tf_op jit(solution)/shard_map/whiten/pallas_call | solution.py:117
  18.6 2.3 %collective-permute-start.3 = (bf16[2,4,48,1024]{3,2,1,0:T(8,128)(2,1)S(1)}, bf16[2,4,48,1024]{3,2,1,0:T(8,128)(2,1)S(1)}, u32[]{:S(2)}, u32[]{:S(2)}) collective-permute-start(bf16[2,4,48,1024]{3,2,1,0:T(8,128)(2,1)S(1)} %whiten.1.mine_ref), channel_id=1, source_target_pairs={{0,1},{1,0},{2,3},{3,2},{4,5},{5,4},{6,7},{7,6},{8,9},{9,8},{10,11... | collective-permute-start | bytes 2359304 | tf_op jit(solution)/shard_map/ppermute | solution.py:331
  20.9 0.0 collective-permute-done.6
  20.9 0.0 collective-permute-done.5
  20.9 0.0 collective-permute-done.4
  21.0 0.1 constant_dynamic-slice_fusion.4
  21.1 3.2 %collective-permute-start.7 = (bf16[2,4,2,1024]{3,1,0,2:T(4,128)(2,1)S(1)}, bf16[2,4,2,1024]{3,1,0,2:T(4,128)(2,1)S(1)}, u32[]{:S(2)}, u32[]{:S(2)}) collective-permute-start(bf16[2,4,2,1024]{3,1,0,2:T(4,128)(2,1)S(1)} %bitcast.76), channel_id=1, source_target_pairs={{0,1},{1,0},{2,3},{3,2},{4,5},{5,4},{6,7},{7,6},{8,9},{9,8},{10,11... | collective-permute-start | bytes 98312 | tf_op jit(solution)/shard_map/ppermute | solution.py:329
  24.3 0.2 broadcast_multiply_fusion
  24.4 0.1 mul.78.member_ref
  24.6 0.5 collective-permute-done.7
  25.2 0.0 collective-permute-done.3.other_ref
  25.2 0.0 copy-done
  25.2 20.7 %stack.25 = bf16[16,8,3,8,256]{4,3,2,1,0:T(8,128)(2,1)} custom-call(bf16[2,4,48,1024]{3,2,1,0:T(8,128)(2,1)S(1)} %whiten.1.mine_ref, bf16[2,4,48,1024]{3,2,1,0:T(8,128)(2,1)S(1)} %collective-permute-done.3.other_ref, bf16[32,1024]{1,0:T(8,128)(2,1)S(1)} %reshape.64.src_ref, bf16[4,1024,1024]{2,1,0:T(8,128)(2,1)} %constant.58.clone.table_ref, ...), custom_call_target="tpu_custom_call" | custom-call | flops 14000000000 | bytes 12000000 | tf_op jit(solution)/shard_map/stack/pallas_call | solution.py:272
  45.9 5.6 %all-to-all-start = ((bf16[64,6,8,256]{3,2,1,0:T(8,128)(2,1)}), bf16[64,6,8,256]{3,2,1,0:T(8,128)(2,1)S(1)}, u32[]{:S(2)}, u32[]{:S(2)}) async-start(bf16[64,6,8,256]{3,2,1,0:T(8,128)(2,1)} %bitcast.9), calls=%async_computation | async-start | bytes 3145728 | tf_op jit(solution)/shard_map/all_to_all | solution.py:344
  51.5 0.1 fusion.9
  51.6 23.6 %all-to-all-done = bf16[64,6,8,256]{3,2,1,0:T(8,128)(2,1)S(1)} async-done(((bf16[64,6,8,256]{3,2,1,0:T(8,128)(2,1)}), bf16[64,6,8,256]{3,2,1,0:T(8,128)(2,1)S(1)}, u32[]{:S(2)}, u32[]{:S(2)}) %all-to-all-start) | async-done | bytes 1572896 | tf_op jit(solution)/shard_map/all_to_all | solution.py:344
  75.2 0.2 convert_reduce_fusion
  75.5 0.1 fusion.6
  75.6 2.0 %collective-permute-start.8 = (f32[2,2,2,256]{3,2,1,0:T(2,128)S(1)}, f32[2,2,2,256]{3,2,1,0:T(2,128)S(1)}, u32[]{:S(2)}, u32[]{:S(2)}) collective-permute-start(f32[2,2,2,256]{3,2,1,0:T(2,128)S(1)} %get-tuple-element.12), channel_id=1, source_target_pairs={{0,1},{1,0},{2,3},{3,2},{4,5},{5,4},{6,7},{7,6},{8,9},{9,8},{10,11... | collective-permute-start | bytes 24584 | tf_op jit(solution)/shard_map/ppermute | solution.py:352
  77.6 0.8 %collective-permute-done.8 = f32[2,2,2,256]{3,2,1,0:T(2,128)S(1)} collective-permute-done((f32[2,2,2,256]{3,2,1,0:T(2,128)S(1)}, f32[2,2,2,256]{3,2,1,0:T(2,128)S(1)}, u32[]{:S(2)}, u32[]{:S(2)}) %collective-permute-start.8) | collective-permute-done | bytes 8224 | tf_op jit(solution)/shard_map/ppermute | solution.py:352
  78.5 0.4 rev.3
  78.9 0.6 broadcast_select_fusion
  (18 shorter events, 0.3 us)
Async XLA Ops:
  2.2 8.6 %copy-start.1 = (bf16[4,4,2,1152]{3,2,1,0:T(2,128)(2,1)S(1)}, bf16[4,4,2,1152]{3,2,1,0:T(2,128)(2,1)}, u32[]{:S(2)}) copy-start(bf16[4,4,2,1152]{3,2,1,0:T(2,128)(2,1)} %pick.1) | copy-start | bytes 221188
  2.2 8.0 %collective-permute-start.2 = (bf16[4,4,2,1152]{3,2,1,0:T(2,128)(2,1)}, bf16[4,4,2,1152]{3,2,1,0:T(2,128)(2,1)S(1)}, u32[]{:S(2)}, u32[]{:S(2)}) collective-permute-start(bf16[4,4,2,1152]{3,2,1,0:T(2,128)(2,1)} %pick.1), channel_id=1, source_target_pairs={{0,16},{1,65},{2,18},{3,67},{4,20},{5,69},{6,22},{7,71},{8,24},{9,... | collective-permute-start | bytes 221192 | tf_op jit(solution)/shard_map/ppermute | solution.py:321
  5.3 4.9 %collective-permute-start.1 = (bf16[4,4,2,1152]{3,2,1,0:T(2,128)(2,1)}, bf16[4,4,2,1152]{3,2,1,0:T(2,128)(2,1)S(1)}, u32[]{:S(2)}, u32[]{:S(2)}) collective-permute-start(bf16[4,4,2,1152]{3,2,1,0:T(2,128)(2,1)} %pick.1), channel_id=1, source_target_pairs={{0,24},{1,97},{2,26},{3,99},{4,28},{5,101},{6,30},{7,103},{8,0},{9... | collective-permute-start | bytes 221192 | tf_op jit(solution)/shard_map/ppermute | solution.py:321
  6.1 4.6 %collective-permute-start = (bf16[4,4,2,1152]{3,2,1,0:T(2,128)(2,1)}, bf16[4,4,2,1152]{3,2,1,0:T(2,128)(2,1)S(1)}, u32[]{:S(2)}, u32[]{:S(2)}) collective-permute-start(bf16[4,4,2,1152]{3,2,1,0:T(2,128)(2,1)} %pick.1), channel_id=1, source_target_pairs={{0,8},{1,33},{2,10},{3,35},{4,12},{5,37},{6,14},{7,39},{8,16},{9,4... | collective-permute-start | bytes 221192 | tf_op jit(solution)/shard_map/ppermute | solution.py:321
  10.8 14.4 %copy-start = (bf16[1024,256]{1,0:T(8,128)(2,1)S(1)}, bf16[1024,256]{1,0:T(8,128)(2,1)}, u32[]{:S(2)}) copy-start(bf16[1024,256]{1,0:T(8,128)(2,1)} %constant.59.clone.edge_table_ref) | copy-start | bytes 1572868
  10.8 10.1 %collective-permute-start.6 = (bf16[4,4,2,1152]{3,2,1,0:T(2,128)(2,1)S(1)}, bf16[4,4,2,1152]{3,2,1,0:T(2,128)(2,1)S(1)}, u32[]{:S(2)}, u32[]{:S(2)}) collective-permute-start(bf16[4,4,2,1152]{3,2,1,0:T(2,128)(2,1)S(1)} %bitcast.61), channel_id=1, source_target_pairs={{0,64},{1,17},{2,66},{3,19},{4,68},{5,21},{6,70},{7,23},{8,72},{9,... | collective-permute-start | bytes 221192 | tf_op jit(solution)/shard_map/ppermute | solution.py:321
  15.1 5.8 %collective-permute-start.5 = (bf16[4,4,2,1152]{3,2,1,0:T(2,128)(2,1)S(1)}, bf16[4,4,2,1152]{3,2,1,0:T(2,128)(2,1)S(1)}, u32[]{:S(2)}, u32[]{:S(2)}) collective-permute-start(bf16[4,4,2,1152]{3,2,1,0:T(2,128)(2,1)S(1)} %bitcast.62), channel_id=1, source_target_pairs={{0,96},{1,25},{2,98},{3,27},{4,100},{5,29},{6,102},{7,31},{8,104},... | collective-permute-start | bytes 221192 | tf_op jit(solution)/shard_map/ppermute | solution.py:321
  15.5 5.4 %collective-permute-start.4 = (bf16[4,4,2,1152]{3,2,1,0:T(2,128)(2,1)S(1)}, bf16[4,4,2,1152]{3,2,1,0:T(2,128)(2,1)S(1)}, u32[]{:S(2)}, u32[]{:S(2)}) collective-permute-start(bf16[4,4,2,1152]{3,2,1,0:T(2,128)(2,1)S(1)} %bitcast.63), channel_id=1, source_target_pairs={{0,32},{1,9},{2,34},{3,11},{4,36},{5,13},{6,38},{7,15},{8,40},{9,1... | collective-permute-start | bytes 221192 | tf_op jit(solution)/shard_map/ppermute | solution.py:321
  18.6 6.6 %collective-permute-start.3 = (bf16[2,4,48,1024]{3,2,1,0:T(8,128)(2,1)S(1)}, bf16[2,4,48,1024]{3,2,1,0:T(8,128)(2,1)S(1)}, u32[]{:S(2)}, u32[]{:S(2)}) collective-permute-start(bf16[2,4,48,1024]{3,2,1,0:T(8,128)(2,1)S(1)} %whiten.1.mine_ref), channel_id=1, source_target_pairs={{0,1},{1,0},{2,3},{3,2},{4,5},{5,4},{6,7},{7,6},{8,9},{9,8},{10,11... | collective-permute-start | bytes 2359304 | tf_op jit(solution)/shard_map/ppermute | solution.py:331
  21.1 4.1 %collective-permute-start.7 = (bf16[2,4,2,1024]{3,1,0,2:T(4,128)(2,1)S(1)}, bf16[2,4,2,1024]{3,1,0,2:T(4,128)(2,1)S(1)}, u32[]{:S(2)}, u32[]{:S(2)}) collective-permute-start(bf16[2,4,2,1024]{3,1,0,2:T(4,128)(2,1)S(1)} %bitcast.76), channel_id=1, source_target_pairs={{0,1},{1,0},{2,3},{3,2},{4,5},{5,4},{6,7},{7,6},{8,9},{9,8},{10,11... | collective-permute-start | bytes 98312 | tf_op jit(solution)/shard_map/ppermute | solution.py:329
  45.9 29.3 %all-to-all-start = ((bf16[64,6,8,256]{3,2,1,0:T(8,128)(2,1)}), bf16[64,6,8,256]{3,2,1,0:T(8,128)(2,1)S(1)}, u32[]{:S(2)}, u32[]{:S(2)}) async-start(bf16[64,6,8,256]{3,2,1,0:T(8,128)(2,1)} %bitcast.9), calls=%async_computation | async-start | bytes 3145728 | tf_op jit(solution)/shard_map/all_to_all | solution.py:344
  75.6 2.8 %collective-permute-start.8 = (f32[2,2,2,256]{3,2,1,0:T(2,128)S(1)}, f32[2,2,2,256]{3,2,1,0:T(2,128)S(1)}, u32[]{:S(2)}, u32[]{:S(2)}) collective-permute-start(f32[2,2,2,256]{3,2,1,0:T(2,128)S(1)} %get-tuple-element.12), channel_id=1, source_target_pairs={{0,1},{1,0},{2,3},{3,2},{4,5},{5,4},{6,7},{7,6},{8,9},{9,8},{10,11... | collective-permute-start | bytes 24584 | tf_op jit(solution)/shard_map/ppermute | solution.py:352
